TPU v7x, 128 devices: a whole 4x4x4 slice. The times are simulated.
128 devices in a mesh: group: 4 (over x), shard: 32 (over z, y, core).
Axes of the slice: x: 4, y: 4, z: 4, core: 2. Of those that a mesh axis runs over, the one named last changes fastest.
Arguments:
- samples: bfloat16 [16384, 1, 4096], P(('group', 'shard')), may hold values from -6 to 6
- fan_taps: float32 [33, 2048], replicated, may hold values from -1 to 1
- pair_blocks: int32 [512, 2], replicated, may hold values from 0 to 127
- pair_valid: int32 [512], P(('group', 'shard')), may hold values 0 or 1
- coil_offsets: int32 [128], replicated, may hold values from 0 to 63
Outputs:
- correlations: float32 [512, 128, 512], P(('group', 'shard'))
Inputs may be any that keep to these rules, and one draw needn't show every extreme that they name: `pair_blocks`: block indices.
All inputs are finite; a program needn't handle non-finite values. No bound on the sum of `pair_valid` on one device may be relied on, other than what follows from the above.
Results may differ from a plain program's by a relative error of at most 0.0076.
Values may be sent and summed in bfloat16 or wider, within the bound.
A program may use at most 192 MiB of HBM per device.

v0:
```python
import jax
import jax.numpy as jnp
from jax import lax
from jax.sharding import PartitionSpec as P

HALF = 16
SMOOTH = 64
NLAG = 512


EPSILON = 1e-05


def with_halo(cells, sides, width):
    for axis, dim in sides:
        count = lax.axis_size(axis)
        ends = count - 1
        head = lax.slice_in_dim(cells, 0, width, axis=dim)
        tail = lax.slice_in_dim(cells, cells.shape[dim] - width, cells.shape[dim], axis=dim)
        cells = jnp.concatenate(
            [
                lax.ppermute(tail, axis, [(i, (i + 1) % count) for i in range(ends)]),
                cells,
                lax.ppermute(head, axis, [((i + 1) % count, i) for i in range(ends)]),
            ],
            axis=dim,
        )
    return cells


def forward_tables(length, bin_count):
    split = 1 << length.bit_length() // 2
    coarse_n = (jnp.arange(length // split, dtype=jnp.int32) * split)[:, None]
    fine_n = jnp.arange(split, dtype=jnp.int32)[:, None]
    cols_k = jnp.arange(bin_count, dtype=jnp.int32)[None, :]
    coarse_ph = jnp.mod(coarse_n * cols_k, length).astype(jnp.float32) * (2.0 * jnp.pi / length)
    fine_ph = jnp.mod(fine_n * cols_k, length).astype(jnp.float32) * (2.0 * jnp.pi / length)
    cos_a = jnp.cos(coarse_ph)[:, None, :]
    sin_a = jnp.sin(coarse_ph)[:, None, :]
    cos_b = jnp.cos(fine_ph)[None, :, :]
    sin_b = jnp.sin(fine_ph)[None, :, :]
    cosine = (cos_a * cos_b - sin_a * sin_b).reshape(length, bin_count)
    sine_vals = (sin_a * cos_b + cos_a * sin_b).reshape(length, bin_count)
    scaled = 1.0 / jnp.sqrt(jnp.float32(length))
    return (jnp.concatenate([cosine, -sine_vals], axis=1) * scaled).astype(jnp.bfloat16)


def inverse_tables(length, bin_count, lag_count):
    freq_index = jnp.arange(bin_count, dtype=jnp.int32)[:, None]
    lagged = jnp.arange(lag_count, dtype=jnp.int32)[None, :] - lag_count // 2
    phases = jnp.mod(freq_index * lagged, length).astype(jnp.float32) * (2.0 * jnp.pi / length)
    return jnp.stack([jnp.cos(phases), -jnp.sin(phases)]).astype(jnp.bfloat16)


def box_mean(power_sum):
    bin_count = power_sum.shape[1]
    zero_row = jnp.zeros_like(power_sum[:, :1])
    prefix = jnp.concatenate([zero_row, jnp.cumsum(power_sum, axis=1)], axis=1)
    last_row = prefix[:, bin_count : bin_count + 1]
    first_row = prefix[:, 0:1]
    upper_vals = jnp.concatenate(
        [
            prefix[:, SMOOTH + 1 :],
            jnp.broadcast_to(last_row, (prefix.shape[0], SMOOTH) + prefix.shape[2:]),
        ],
        axis=1,
    )
    lower_vals = jnp.concatenate(
        [
            jnp.broadcast_to(first_row, (prefix.shape[0], SMOOTH + 1) + prefix.shape[2:]),
            prefix[:, 1 : bin_count - SMOOTH],
        ],
        axis=1,
    )
    bins_k = jnp.arange(bin_count, dtype=jnp.int32)
    counts = (
        jnp.minimum(bins_k + SMOOTH, bin_count - 1) - jnp.maximum(bins_k - SMOOTH, 0) + 1
    ).astype(jnp.float32)
    return (upper_vals - lower_vals) / counts[None, :, None]


def whiten(padded, fan_taps):
    width = padded.shape[3] - 2 * HALF
    filtered = jnp.zeros(padded.shape[:3] + (width,), jnp.float32)
    for offset in range(2 * HALF + 1):
        filtered = filtered + fan_taps[offset][None, None, :, None] * padded[
            :, :, :, offset : offset + width
        ].astype(jnp.float32)
    power_sum = filtered[:, 0] * filtered[:, 0] + filtered[:, 1] * filtered[:, 1]
    mean_power = box_mean(power_sum)
    return (filtered * lax.rsqrt(mean_power + EPSILON)[:, None]).astype(jnp.bfloat16)


def body(samples, fan_taps, pair_blocks, pair_valid, coil_offsets):
    block_width = samples.shape[0]
    segments = samples.shape[1]
    length = samples.shape[2]
    bin_count = length // 2
    groups = lax.axis_size("group")
    shards = lax.axis_size("shard")
    devices = groups * shards
    bins_device = bin_count // devices
    forward = forward_tables(length, bin_count)
    spectra = jnp.einsum("cst,tk->skc", samples, forward, preferred_element_type=jnp.float32)
    padded = with_halo(
        spectra.astype(jnp.bfloat16).reshape(segments, 2, bin_count, samples.shape[0]),
        ((("group", "shard"), 3),),
        HALF,
    )
    whitened = whiten(padded, fan_taps)
    banded = lax.all_to_all(whitened, ("group", "shard"), split_axis=2, concat_axis=3, tiled=True)
    first_block = pair_blocks[:, 0]
    second_block = pair_blocks[:, 1]
    blocks = banded.reshape(segments, 2, bins_device, devices, block_width)
    rolled = jnp.roll(blocks, -(block_width // 2), axis=4)
    left_side = jnp.take(blocks, first_block, axis=3)
    right_side = jnp.take(rolled, second_block, axis=3)
    form = "skpc,skpc->kpc"
    real_part = jnp.einsum(
        form, left_side[:, 0], right_side[:, 0], preferred_element_type=jnp.float32
    ) + jnp.einsum(form, left_side[:, 1], right_side[:, 1], preferred_element_type=jnp.float32)
    imag_part = jnp.einsum(
        form, left_side[:, 1], right_side[:, 0], preferred_element_type=jnp.float32
    ) - jnp.einsum(form, left_side[:, 0], right_side[:, 1], preferred_element_type=jnp.float32)
    block_ids = jnp.arange(devices, dtype=jnp.int32)[None, :]
    first_offset = jnp.sum(
        jnp.where(first_block[:, None] == block_ids, coil_offsets[None, :], 0), axis=1
    )
    second_offset = jnp.sum(
        jnp.where(second_block[:, None] == block_ids, coil_offsets[None, :], 0), axis=1
    )
    shift_samples = first_offset - second_offset
    bin_index = lax.axis_index(("group", "shard")) * bins_device + jnp.arange(
        bins_device, dtype=jnp.int32
    )
    phases = jnp.mod(bin_index[:, None] * shift_samples[None, :], length).astype(jnp.float32) * (
        2.0 * jnp.pi / length
    )
    cosine = jnp.cos(phases)[:, :, None]
    sine_values = jnp.sin(phases)[:, :, None]
    cross_spec = jnp.stack(
        [real_part * cosine + imag_part * sine_values, imag_part * cosine - real_part * sine_values]
    ).astype(jnp.bfloat16)
    owned_spec = lax.all_to_all(
        cross_spec, ("group", "shard"), split_axis=2, concat_axis=1, tiled=True
    )
    inverse = inverse_tables(length, bin_count, NLAG)
    correlations = jnp.einsum(
        "rkpc,rkl->pcl", owned_spec, inverse, preferred_element_type=jnp.float32
    )
    weights = pair_valid.astype(jnp.float32) / jnp.sqrt(jnp.float32(bin_count * segments))
    return correlations * weights[:, None, None]


def solution(mesh):
    return jax.shard_map(
        body,
        mesh=mesh,
        in_specs=(P(("group", "shard"), None, None), P(), P(), P(("group", "shard")), P()),
        out_specs=P(("group", "shard"), None, None),
        check_vma=False,
    )
```

profile of v0, /device:TPU:1, one launch (start us, length us, event | category | flops | bytes accessed | tf_op | source)
XLA Modules:
  0.0 236.7 jit_solution(15228262035999444965)
XLA Ops:
  0.0 2.0 fusion.74
  2.1 2.1 fusion.77
  4.2 22.0 %multiply_subtract_fusion = (f32[64,64,2048]{2,1,0:T(8,128)}, f32[64,64,2048]{2,1,0:T(8,128)}) fusion(f32[64,2048]{1,0:T(8,128)S(1)} %get-tuple-element.57, f32[64,2048]{1,0:T(8,128)S(1)} %get-tuple-element.56, f32[64,2048]{1,0:T(8,128)S(1)} %get-tuple-element.58, f32[64,2048]{1,0:T(8,128)S(1)} %get-tuple-element.55), kind=kLoop, calls=%fused_computation.5 | loop fusion | flops 58720256 | bytes 69206016 | tf_op jit(solution)/shard_map/sub | solution.py:42
  26.2 22.9 %fusion.3 = bf16[4096,128]{1,0:T(8,128)(2,1)S(1)} fusion(f32[4096,2048]{1,0:T(8,128)} %bitcast.155, f32[4096,2048]{1,0:T(8,128)} %bitcast.154, bf16[128,1,4096]{2,0,1:T(8,128)(2,1)S(1)} %copy-done), kind=kOutput, calls=%fused_computation.76 | convolution fusion | flops 4345823232 | bytes 69206016 | tf_op jit(solution)/shard_map/cst,tk->skc/dot_general | solution.py:104
  49.2 0.4 fusion.92
  49.5 0.6 copy-done.3
  50.1 0.3 copy.61
  50.4 4.6 %collective-permute-start = (bf16[1,2,2048,16]{2,3,1,0:T(8,128)(2,1)S(1)}, bf16[1,2,2048,16]{2,3,1,0:T(8,128)(2,1)S(1)}, u32[]{:S(2)}, u32[]{:S(2)}) collective-permute-start(bf16[1,2,2048,16]{2,3,1,0:T(8,128)(2,1)S(1)} %copy.61), channel_id=1, source_target_pairs={{0,1},{1,2},{2,3},{3,4},{4,5},{5,6},{6,7},{7,8},{8,9},{9,10},{10,1... | collective-permute-start | bytes 393224 | tf_op jit(solution)/shard_map/ppermute | solution.py:22
  55.0 0.3 copy.63
  55.3 2.2 collective-permute-start.1
  57.6 0.7 fusion.93
  58.3 0.7 fusion.94
  59.2 0.4 select_reduce_fusion
  59.5 0.2 copy-done.17
  59.7 0.2 fusion.82
  59.9 0.1 copy.72
  60.1 0.9 copy.75
  60.9 0.6 fusion.86
  61.5 1.3 copy.62
  62.9 1.3 copy.64
  64.3 40.0 %multiply_add_fusion = f32[1,2,2048,128]{3,2,1,0:T(8,128)S(1)} fusion(bf16[1,2,2048,128]{3,2,1,0:T(8,128)(2,1)S(1)} %bitcast.157, bf16[1,2,2048,16]{3,2,1,0:T(8,128)(2,1)} %copy.64, bf16[1,2,2048,16]{3,2,1,0:T(8,128)(2,1)} %copy.62, f32[2048]{0:T(1024)} %bitcast.194, f32[2048]{0:T(1024)} %bitcast.195, f32[2048]{0:T(1024)S(1)} %bitcast.164, ...), kind=kLoop, calls=%fused_computation.103 | loop fusion | flops 101711872 | bytes 3678208 | tf_op jit(solution)/shard_map/add | solution.py:86
  104.2 0.1 fusion.54
  104.3 0.6 fusion.60
  105.0 1.3 copy.66
  106.3 1.3 bitcast_add_fusion
  107.6 0.1 slice.438
  107.7 0.1 slice.440
  107.8 0.5 copy-done.16
  108.3 0.4 fusion.58
  108.7 0.2 multiply_convert_fusion
  108.9 9.5 %copy.67 = bf16[1,2,2048,128]{3,1,0,2:T(2,128)(2,1)} copy(bf16[1,2,2048,128]{3,2,1,0:T(8,128)(2,1)S(1)} %multiply_convert_fusion) | data formatting | bytes 2097152 | tf_op jit(solution)/shard_map/convert_element_type | solution.py:91
  118.3 11.2 %all-to-all-start = ((bf16[1,2,2048,128]{3,1,0,2:T(2,128)(2,1)}), bf16[1,2,2048,128]{3,1,0,2:T(2,128)(2,1)S(1)}, u32[]{:S(2)}, u32[]{:S(2)}) async-start(bf16[1,2,2048,128]{3,1,0,2:T(2,128)(2,1)} %copy.67), calls=%async_computation | async-start | bytes 2097152 | tf_op jit(solution)/shard_map/all_to_all | solution.py:111
  129.6 19.0 %all-to-all-done = bf16[1,2,2048,128]{3,1,0,2:T(2,128)(2,1)S(1)} async-done(((bf16[1,2,2048,128]{3,1,0,2:T(2,128)(2,1)}), bf16[1,2,2048,128]{3,1,0,2:T(2,128)(2,1)S(1)}, u32[]{:S(2)}, u32[]{:S(2)}) %all-to-all-start) | async-done | bytes 1048608 | tf_op jit(solution)/shard_map/all_to_all | solution.py:111
  148.6 0.1 copy.68
  148.7 0.5 fusion.91
  149.2 0.6 maximum_bitcast_fusion.6
  149.8 3.5 %gather_fusion.1 = bf16[512,2,16,128]{3,2,1,0:T(8,128)(2,1)} fusion(bf16[2,16,128,128]{3,1,2,0:T(8,128)(2,1)S(1)} %maximum_bitcast_fusion.6, s32[1024]{0:T(1024)S(1)} %pad_clamp_fusion), kind=kCustom, calls=%fused_computation.1.clone | custom fusion | bytes 8390656 | tf_op jit(solution)/shard_map/jit(_take)/gather | solution.py:117
  153.3 4.6 %bitcast_select_fusion = bf16[1,2,16,512,128]{4,2,3,1,0:T(8,128)(2,1)} fusion(bf16[512,2,16,128]{3,2,1,0:T(8,128)(2,1)} %gather_fusion.1, pred[512]{0:T(512)(128)(4,1)S(1)} %compare_and_fusion), kind=kLoop, calls=%fused_computation.90 | loop fusion | flops 2097152 | bytes 8389120 | tf_op jit(solution)/shard_map/jit(_take)/select_n | solution.py:117
  157.9 3.5 %gather_fusion = bf16[512,2,16,128]{3,2,1,0:T(8,128)(2,1)} fusion(bf16[2,16,128,128]{3,1,2,0:T(8,128)(2,1)S(1)} %bitcast.153, s32[1024]{0:T(1024)S(1)} %pad_clamp_fusion.1), kind=kCustom, calls=%fused_computation.clone | custom fusion | bytes 8390656 | tf_op jit(solution)/shard_map/jit(_take)/gather | solution.py:116
  161.4 3.4 %bitcast_select_fusion.1 = bf16[1,2,16,512,128]{4,2,1,3,0:T(8,128)(2,1)S(1)} fusion(bf16[512,2,16,128]{3,2,1,0:T(8,128)(2,1)} %gather_fusion, pred[512]{0:T(512)(128)(4,1)S(1)} %compare_and_fusion.1), kind=kLoop, calls=%fused_computation.91 | loop fusion | flops 2097152 | bytes 8389120 | tf_op jit(solution)/shard_map/jit(_take)/select_n | solution.py:116
  164.9 3.6 %fusion.20 = (bf16[1,16,512,128]{3,1,2,0:T(8,128)(2,1)S(1)}, bf16[1,16,512,128]{3,1,2,0:T(8,128)(2,1)S(1)}) fusion(f32[16,512]{0,1:T(8,128)S(1)} %copy-done.6, f32[16,512]{0,1:T(8,128)S(1)} %copy.72, bf16[1,2,16,512,128]{4,2,3,1,0:T(8,128)(2,1)S(1)} %copy-done.2, bf16[1,2,16,512,128]{4,2,1,3,0:T(8,128)(2,1)S(1)} %bitcast_select_fusion.1), kind=kLoop, calls=%fused_computation.99 | loop fusion | flops 18874368 | bytes 12648448 | tf_op jit(solution)/shard_map/stack | solution.py:141
  168.5 0.4 pad_maximum_fusion
  168.9 2.7 %copy.76 = bf16[2,16,512,128]{3,1,0,2:T(8,128)(2,1)} copy(bf16[2,16,512,128]{3,1,2,0:T(8,128)(2,1)S(1)} %pad_maximum_fusion) | data formatting | bytes 8388608 | tf_op jit(solution)/shard_map/stack | solution.py:141
  171.7 5.8 %all-to-all-start.1 = ((bf16[2,16,512,128]{3,1,0,2:T(8,128)(2,1)}), bf16[2,16,512,128]{3,1,0,2:T(8,128)(2,1)}, u32[]{:S(2)}, u32[]{:S(2)}) async-start(bf16[2,16,512,128]{3,1,0,2:T(8,128)(2,1)} %copy.76), calls=%async_computation.1 | async-start | bytes 8388608 | tf_op jit(solution)/shard_map/all_to_all | solution.py:144
  177.5 18.2 %cosine_convert_fusion = (bf16[1,2048,512]{2,1,0:T(8,128)(2,1)S(1)}, bf16[1,2048,512]{2,1,0:T(8,128)(2,1)}) fusion(s32[512]{0:T(512)S(1)} %iota_add_fusion.2), kind=kLoop, calls=%fused_computation.93 | loop fusion | flops 17825792 | bytes 4196352 | tf_op jit(solution)/shard_map/convert.12
  195.7 34.5 %all-to-all-done.1 = bf16[2,16,512,128]{3,1,0,2:T(8,128)(2,1)} async-done(((bf16[2,16,512,128]{3,1,0,2:T(8,128)(2,1)}), bf16[2,16,512,128]{3,1,0,2:T(8,128)(2,1)}, u32[]{:S(2)}, u32[]{:S(2)}) %all-to-all-start.1) | async-done | bytes 4194336 | tf_op jit(solution)/shard_map/all_to_all | solution.py:144
  230.2 3.1 %copy.78 = bf16[2,128,16,4,128]{4,2,1,3,0:T(8,128)(2,1)S(1)} copy(bf16[2,128,16,4,128]{4,2,0,3,1:T(8,128)(2,1)} %bitcast.67) | data formatting | bytes 8388608 | tf_op jit(solution)/shard_map/all_to_all | solution.py:144
  233.3 3.3 %fusion.23 = f32[4,128,512]{2,1,0:T(8,128)} fusion(bf16[2,2048,4,128]{3,1,2,0:T(8,128)(2,1)S(1)} %bitcast.162, bf16[1,2048,512]{2,1,0:T(8,128)(2,1)S(1)} %copy-done.5, bf16[1,2048,512]{2,1,0:T(8,128)(2,1)S(1)} %get-tuple-element.53, f32[4]{0:T(128)S(1)} %convert_multiply_fusion.4), kind=kOutput, calls=%fused_computation.105 | convolution fusion | flops 2149842944 | bytes 9437200 | tf_op jit(solution)/shard_map/rkpc,rkl->pcl/dot_general | solution.py:148
  (64 shorter events, 0.3 us)
Async XLA Ops:
  0.0 26.2 %copy-start = (bf16[128,1,4096]{2,0,1:T(8,128)(2,1)S(1)}, bf16[128,1,4096]{2,0,1:T(8,128)(2,1)}, u32[]{:S(2)}) copy-start(bf16[128,1,4096]{2,0,1:T(8,128)(2,1)} %param.7) | copy-start | bytes 3145732
  49.1 1.0 copy-start.3
  50.1 7.5 %copy-start.7 = (f32[33,2048]{1,0:T(8,128)S(1)}, f32[33,2048]{1,0:T(8,128)}, u32[]{:S(2)}) copy-start(f32[33,2048]{1,0:T(8,128)} %param.8) | copy-start | bytes 811012
  50.1 9.0 %copy-start.21 = (s32[512,2]{0,1:T(2,128)S(1)}, s32[512,2]{0,1:T(2,128)}, u32[]{:S(2)}) copy-start(s32[512,2]{0,1:T(2,128)} %param.9) | copy-start | bytes 12292
  50.1 9.0 %copy-start.22 = (s32[128]{0:T(128)S(1)}, s32[128]{0:T(128)}, u32[]{:S(2)}) copy-start(s32[128]{0:T(128)} %param.11) | copy-start | bytes 1540
  50.4 11.1 %collective-permute-start = (bf16[1,2,2048,16]{2,3,1,0:T(8,128)(2,1)S(1)}, bf16[1,2,2048,16]{2,3,1,0:T(8,128)(2,1)S(1)}, u32[]{:S(2)}, u32[]{:S(2)}) collective-permute-start(bf16[1,2,2048,16]{2,3,1,0:T(8,128)(2,1)S(1)} %copy.61), channel_id=1, source_target_pairs={{0,1},{1,2},{2,3},{3,4},{4,5},{5,6},{6,7},{7,8},{8,9},{9,10},{10,1... | collective-permute-start | bytes 393224 | tf_op jit(solution)/shard_map/ppermute | solution.py:22
  55.3 8.8 %copy-start.4 = (bf16[4096,128]{1,0:T(8,128)(2,1)S(1)}, bf16[4096,128]{1,0:T(8,128)(2,1)}, u32[]{:S(2)}) copy-start(bf16[4096,128]{1,0:T(8,128)(2,1)} %copy-done.3) | copy-start | bytes 3145732
  55.3 7.5 %collective-permute-start.1 = (bf16[1,2,2048,16]{2,3,1,0:T(8,128)(2,1)S(1)}, bf16[1,2,2048,16]{2,3,1,0:T(8,128)(2,1)S(1)}, u32[]{:S(2)}, u32[]{:S(2)}) collective-permute-start(bf16[1,2,2048,16]{2,3,1,0:T(8,128)(2,1)S(1)} %copy.63), channel_id=1, source_target_pairs={{1,0},{2,1},{3,2},{4,3},{5,4},{6,5},{7,6},{8,7},{9,8},{10,9},{11,1... | collective-permute-start | bytes 393224 | tf_op jit(solution)/shard_map/ppermute | solution.py:24
  59.0 5.2 %copy-start.8 = (f32[1,2048]{1,0:T(1,128)S(1)}, f32[1,2048]{1,0:T(1,128)}, u32[]{:S(2)}) copy-start(f32[1,2048]{1,0:T(1,128)} %get-tuple-element.26) | copy-start | bytes 24580
  59.0 5.2 %copy-start.9 = (f32[1,2048]{1,0:T(1,128)S(1)}, f32[1,2048]{1,0:T(1,128)}, u32[]{:S(2)}) copy-start(f32[1,2048]{1,0:T(1,128)} %get-tuple-element.27) | copy-start | bytes 24580
  59.0 5.2 %copy-start.10 = (f32[1,2048]{1,0:T(1,128)S(1)}, f32[1,2048]{1,0:T(1,128)}, u32[]{:S(2)}) copy-start(f32[1,2048]{1,0:T(1,128)} %get-tuple-element.28) | copy-start | bytes 24580
  59.1 5.2 %copy-start.11 = (f32[1,2048]{1,0:T(1,128)S(1)}, f32[1,2048]{1,0:T(1,128)}, u32[]{:S(2)}) copy-start(f32[1,2048]{1,0:T(1,128)} %get-tuple-element.29) | copy-start | bytes 24580
  59.1 5.2 %copy-start.12 = (f32[1,2048]{1,0:T(1,128)S(1)}, f32[1,2048]{1,0:T(1,128)}, u32[]{:S(2)}) copy-start(f32[1,2048]{1,0:T(1,128)} %get-tuple-element.30) | copy-start | bytes 24580
  59.1 5.2 %copy-start.13 = (f32[1,2048]{1,0:T(1,128)S(1)}, f32[1,2048]{1,0:T(1,128)}, u32[]{:S(2)}) copy-start(f32[1,2048]{1,0:T(1,128)} %get-tuple-element.31) | copy-start | bytes 24580
  59.1 5.2 %copy-start.14 = (f32[1,2048]{1,0:T(1,128)S(1)}, f32[1,2048]{1,0:T(1,128)}, u32[]{:S(2)}) copy-start(f32[1,2048]{1,0:T(1,128)} %get-tuple-element.32) | copy-start | bytes 24580
  59.1 5.2 %copy-start.15 = (f32[1,2048]{1,0:T(1,128)S(1)}, f32[1,2048]{1,0:T(1,128)}, u32[]{:S(2)}) copy-start(f32[1,2048]{1,0:T(1,128)} %get-tuple-element.33) | copy-start | bytes 24580
  59.1 0.6 copy-start.17
  59.1 0.6 copy-start.19
  107.6 0.7 copy-start.16
  108.8 20.7 %copy-start.20 = (s32[512,1]{0,1:T(1,128)S(1)}, s32[512,1]{0,1:T(1,128)}, u32[]{:S(2)}) copy-start(s32[512,1]{0,1:T(1,128)} %copy-done.19) | copy-start | bytes 6148
  108.8 20.7 %copy-start.18 = (s32[512,1]{0,1:T(1,128)S(1)}, s32[512,1]{0,1:T(1,128)}, u32[]{:S(2)}) copy-start(s32[512,1]{0,1:T(1,128)} %copy-done.17) | copy-start | bytes 6148
  118.3 30.3 %all-to-all-start = ((bf16[1,2,2048,128]{3,1,0,2:T(2,128)(2,1)}), bf16[1,2,2048,128]{3,1,0,2:T(2,128)(2,1)S(1)}, u32[]{:S(2)}, u32[]{:S(2)}) async-start(bf16[1,2,2048,128]{3,1,0,2:T(2,128)(2,1)} %copy.67), calls=%async_computation | async-start | bytes 2097152 | tf_op jit(solution)/shard_map/all_to_all | solution.py:111
  161.4 3.4 %copy-start.2 = (bf16[1,2,16,512,128]{4,2,3,1,0:T(8,128)(2,1)S(1)}, bf16[1,2,16,512,128]{4,2,3,1,0:T(8,128)(2,1)}, u32[]{:S(2)}) copy-start(bf16[1,2,16,512,128]{4,2,3,1,0:T(8,128)(2,1)} %bitcast_select_fusion) | copy-start | bytes 12582916
  161.4 3.5 %copy-start.6 = (f32[16,512]{0,1:T(8,128)S(1)}, f32[16,512]{0,1:T(8,128)}, u32[]{:S(2)}) copy-start(f32[16,512]{0,1:T(8,128)} %copy.75) | copy-start | bytes 98308
  171.7 5.9 %copy-start.23 = (s32[4]{0:T(128)S(1)}, s32[4]{0:T(128)}, u32[]{:S(2)}) copy-start(s32[4]{0:T(128)} %param.10) | copy-start | bytes 52
  171.7 58.5 %all-to-all-start.1 = ((bf16[2,16,512,128]{3,1,0,2:T(8,128)(2,1)}), bf16[2,16,512,128]{3,1,0,2:T(8,128)(2,1)}, u32[]{:S(2)}, u32[]{:S(2)}) async-start(bf16[2,16,512,128]{3,1,0,2:T(8,128)(2,1)} %copy.76), calls=%async_computation.1 | async-start | bytes 8388608 | tf_op jit(solution)/shard_map/all_to_all | solution.py:144
  230.2 3.1 %copy-start.5 = (bf16[1,2048,512]{2,1,0:T(8,128)(2,1)S(1)}, bf16[1,2048,512]{2,1,0:T(8,128)(2,1)}, u32[]{:S(2)}) copy-start(bf16[1,2048,512]{2,1,0:T(8,128)(2,1)} %get-tuple-element.54) | copy-start | bytes 6291460
  233.3 3.4 %copy-start.1 = (bf16[128,1,4096]{2,0,1:T(8,128)(2,1)S(1)}, bf16[128,1,4096]{2,0,1:T(8,128)(2,1)}, u32[]{:S(2)}) copy-start(bf16[128,1,4096]{2,0,1:T(8,128)(2,1)} %param.7) | copy-start | bytes 3145732
where the time goes:
time: 237 us
  other arithmetic  101 us (43%)
  waiting for transfers between devices  53.4 us (23%)
  local copies, waits for them, and re-layouts  31.9 us (13%)
  matrix products  26.3 us (11%)
  starting transfers between devices  23.9 us (10%)
    add x1, other arithmetic, whiten(): filtered + fan_taps[offset][None, None, :, None] * padded[:, :, :, offset...  40 us
    all_to_all x1, waiting for transfers between devices, body(): lax.all_to_all(cross_spec, ('group', 'shard'), split_axis=2, concat_axis=...  34.5 us
    dot_general x1, matrix products, body(): jnp.einsum('cst,tk->skc', samples, forward, preferred_element_type=jnp.fl...  22.9 us
    sub x1, other arithmetic, forward_tables(): cosine = (cos_a * cos_b - sin_a * sin_b).reshape(length, bin_count)  22 us
    another operation x4, other arithmetic  20.1 us
    all_to_all x1, waiting for transfers between devices, body(): lax.all_to_all(whitened, ('group', 'shard'), split_axis=2, concat_axis=3,...  19 us
    all_to_all x1, starting transfers between devices, body(): lax.all_to_all(whitened, ('group', 'shard'), split_axis=2, concat_axis=3,...  11.2 us
    convert_element_type x1, local copies, waits for them, and re-layouts, whiten(): (filtered * lax.rsqrt(mean_power + EPSILON)[:, None]).astype(jnp.bfloat16)  9.46 us
  transfers between devices with their start and end apart: 4, of which 2 were waited for; matrix products, arithmetic and copies ran while one was open for 10% of the time, Pallas kernels for 0%

commit v1 on v0

v1 whole, which is shorter than its diff:
```python
import functools
import math

import jax
import jax.numpy as jnp
import ml_dtypes
import numpy as np
from jax import lax
from jax.experimental import pallas as pl
from jax.experimental.pallas import tpu as pltpu
from jax.sharding import PartitionSpec as P

HALF = 16
NLAG = 512
NT = 4096
NB = 2048
BLK = 128
WIDE = BLK + 2 * HALF
EPSILON = 1e-05
AXES = ("group", "shard")
NDEV = 128
TAPS = 2 * HALF + 1
QT = 16


def residues():
    low = np.arange(QT)
    high = np.where(low == 0, 16, 32 - low)
    return low, high


def tile_bins():
    low, high = residues()
    k2 = np.arange(64)
    return np.concatenate([low[:, None] + 32 * k2, high[:, None] + 32 * k2], axis=1)


def second_stage_table():
    bins = tile_bins()
    b = np.arange(128)
    phase = 2 * np.pi * ((b[None, :, None] * bins[:, None, :]) % NT) / NT
    cos, sin = np.cos(phase), np.sin(phase)
    table = np.zeros((QT, 2, 128, 2, 128))
    conj = np.concatenate([np.ones(64), -np.ones(64)])
    table[:, 0, :, 0] = cos
    table[:, 1, :, 0] = sin * conj
    table[:, 0, :, 1] = -sin
    table[:, 1, :, 1] = cos * conj
    table[0] = 0.0
    table[0, 0, :, 0, :64] = cos[0, :, :64]
    table[0, 0, :, 1, :64] = -sin[0, :, :64]
    table[0, 1, :, 0, 64:] = cos[0, :, 64:]
    table[0, 1, :, 1, 64:] = -sin[0, :, 64:]
    return (table.reshape(QT, 256, 256) / math.sqrt(NT)).astype(ml_dtypes.bfloat16)


def inverse_table():
    bins = tile_bins().reshape(NDEV, 16)
    lags = np.arange(NLAG) - NLAG // 2
    phase = 2 * np.pi * ((bins[:, :, None] * lags) % NT) / NT
    return np.stack([np.cos(phase), -np.sin(phase)], axis=1).astype(ml_dtypes.bfloat16)


def real_fft(rows):
    count = len(rows)
    if count == 2:
        return [(rows[0] + rows[1], None), (rows[0] - rows[1], None)]
    even = real_fft(rows[0::2])
    odd = real_fft(rows[1::2])
    half, quarter = count // 2, count // 4
    out = [None] * (half + 1)
    out[0] = (even[0][0] + odd[0][0], None)
    out[half] = (even[0][0] - odd[0][0], None)
    out[quarter] = (even[quarter][0], -odd[quarter][0])
    for k in range(1, quarter):
        wr, wi = math.cos(2 * math.pi * k / count), -math.sin(2 * math.pi * k / count)
        o_re, o_im = odd[k]
        e_re, e_im = even[k]
        t_re = o_re * wr - o_im * wi
        t_im = o_re * wi + o_im * wr
        out[k] = (e_re + t_re, e_im + t_im)
        out[half - k] = (e_re - t_re, t_im - e_im)
    return out


def white_kernel(x_ref, table_ref, taps_ref, offsets_ref, out_ref, y_ref, spec_ref, filt_ref, run_ref, rows_ref):
    me = lax.axis_index("group") * lax.axis_size("shard") + lax.axis_index("shard")

    lane = lax.broadcasted_iota(jnp.int32, (QT, 128), 1)
    tile = lax.broadcasted_iota(jnp.int32, (QT, 128), 0)
    residue = jnp.where(lane < 64, tile, jnp.where(tile == 0, 16, 32 - tile))
    bins = residue + 32 * (lane & 63)
    theta = ((bins * offsets_ref[me]) & (NT - 1)).astype(jnp.float32) * (2.0 * math.pi / NT)
    rows_ref[0] = jnp.cos(theta)
    rows_ref[1] = jnp.sin(theta)
    count = jnp.minimum(bins + 64, NB - 1) - jnp.maximum(bins - 64, 0) + 1
    rows_ref[2] = 1.0 / count.astype(jnp.float32)

    @pl.loop(0, WIDE // 16)
    def _(chunk):
        at = pl.ds(pl.multiple_of(chunk * 16, 16), 16)
        rows = [x_ref[at, a * 128 : (a + 1) * 128].astype(jnp.float32) for a in range(32)]
        freq = real_fft(rows)
        for q in range(QT):
            first = freq[q][0]
            second = freq[16][0] if q == 0 else freq[q][1]
            y_ref[q, at, 0:128] = first.astype(jnp.bfloat16)
            y_ref[q, at, 128:256] = second.astype(jnp.bfloat16)

    @pl.loop(0, QT)
    def _(q):
        both = jnp.dot(y_ref[q], table_ref[q], preferred_element_type=jnp.float32)
        spec_ref[q, 0] = both[:, :128]
        spec_ref[q, 1] = both[:, 128:]

    run_ref[...] = jnp.zeros_like(run_ref)

    @pl.loop(0, QT)
    def _(q):
        def tap_step(t, sums):
            re, im = sums
            tap = taps_ref[q, pl.ds(t, 1), :]
            re = re + tap * spec_ref[q, 0, pl.ds(t, BLK), :]
            im = im + tap * spec_ref[q, 1, pl.ds(t, BLK), :]
            return re, im

        zero = jnp.zeros((BLK, 128), jnp.float32)
        re, im = lax.fori_loop(0, TAPS, tap_step, (zero, zero), unroll=3)
        filt_ref[q, 0] = re
        filt_ref[q, 1] = im
        run_ref[0] += re * re + im * im

    lanes = lax.broadcasted_iota(jnp.int32, (BLK, 128), 1)
    low = lanes < 64
    k2 = lanes & 63
    sums = run_ref[0]
    swapped = pltpu.roll(sums, 64, 1)
    total = sums + swapped
    run_ref[1] = total
    run_ref[2] = (
        total
        + jnp.where(k2 >= 1, pltpu.roll(total, 1, 1), 0.0)
        + jnp.where(k2 <= 62, pltpu.roll(total, 127, 1), 0.0)
    )

    def finish(q, re, im, prefix, suffix):
        window = (
            run_ref[2]
            + jnp.where(k2 >= 2, pltpu.roll(suffix, 2, 1), 0.0)
            + jnp.where(k2 <= 61, pltpu.roll(prefix, 126, 1), 0.0)
        )
        scale = lax.rsqrt(window * rows_ref[2, pl.ds(q, 1), :] + EPSILON)
        cos = rows_ref[0, pl.ds(q, 1), :]
        sin = rows_ref[1, pl.ds(q, 1), :]
        white_re = ((re * cos + im * sin) * scale).astype(jnp.bfloat16).T
        white_im = ((im * cos - re * sin) * scale).astype(jnp.bfloat16).T
        bands = pl.ds(q * 8, 8)
        out_ref[bands, 0] = white_re.reshape(8, 16, 128)
        out_ref[bands, 1] = white_im.reshape(8, 16, 128)

    re, im = filt_ref[0, 0], filt_ref[0, 1]
    power = re * re + im * im
    finish(0, re, im, jnp.where(low, power, swapped + power), jnp.where(low, total, sums))
    run_ref[0] = jnp.where(low, power, 0.0)

    @pl.loop(1, QT)
    def _(q):
        re, im = filt_ref[q, 0], filt_ref[q, 1]
        before = run_ref[0]
        upto = before + (re * re + im * im)
        rest = jnp.maximum(run_ref[1] - before, 0.0)
        run_ref[0] = upto
        finish(q, re, im, jnp.where(low, upto, rest), jnp.where(low, rest, upto))


def whiten_block(wide, table, taps, offsets):
    return pl.pallas_call(
        white_kernel,
        out_shape=jax.ShapeDtypeStruct((NDEV, 2, 16, BLK), jnp.bfloat16),
        in_specs=[
            pl.BlockSpec(memory_space=pltpu.VMEM),
            pl.BlockSpec(memory_space=pltpu.VMEM),
            pl.BlockSpec(memory_space=pltpu.VMEM),
            pl.BlockSpec(memory_space=pltpu.SMEM),
        ],
        out_specs=pl.BlockSpec(memory_space=pltpu.VMEM),
        scratch_shapes=[
            pltpu.VMEM((QT, WIDE, 256), jnp.bfloat16),
            pltpu.VMEM((QT, 2, WIDE, 128), jnp.float32),
            pltpu.VMEM((QT, 2, BLK, 128), jnp.float32),
            pltpu.VMEM((3, BLK, 128), jnp.float32),
            pltpu.VMEM((3, QT, 128), jnp.float32),
        ],
        compiler_params=pltpu.CompilerParams(vmem_limit_bytes=40 << 20),
        name="whiten_block",
    )(wide, table, taps, offsets)


def cross_kernel(step, pairs_ref, bands_ref, out_ref, rolled_ref):
    i = pl.program_id(0)

    @pl.when(i == 0)
    def _():
        @pl.loop(0, NDEV)
        def _(block):
            both = bands_ref[block].astype(jnp.float32).reshape(32, 128)
            rolled_ref[block] = pltpu.roll(both, 64, 1).astype(jnp.bfloat16).reshape(2, 16, 128)

    @pl.loop(0, step, unroll=4)
    def _(p):
        a = pairs_ref[2 * (i * step + p)]
        b = pairs_ref[2 * (i * step + p) + 1]
        left = bands_ref[a].astype(jnp.float32)
        right = rolled_ref[b].astype(jnp.float32)
        out_ref[p, 0] = (left[0] * right[0] + left[1] * right[1]).astype(jnp.bfloat16)
        out_ref[p, 1] = (left[1] * right[0] - left[0] * right[1]).astype(jnp.bfloat16)


def cross_products(pairs, bands):
    count = pairs.shape[0] // 2
    step = count // 8
    return pl.pallas_call(
        functools.partial(cross_kernel, step),
        out_shape=jax.ShapeDtypeStruct((count, 2, 16, BLK), jnp.bfloat16),
        grid_spec=pltpu.PrefetchScalarGridSpec(
            num_scalar_prefetch=1,
            grid=(8,),
            in_specs=[pl.BlockSpec((NDEV, 2, 16, BLK), lambda i, *_: (0, 0, 0, 0))],
            out_specs=pl.BlockSpec((step, 2, 16, BLK), lambda i, *_: (i, 0, 0, 0)),
            scratch_shapes=[pltpu.VMEM((NDEV, 2, 16, BLK), jnp.bfloat16)],
        ),
        compiler_params=pltpu.CompilerParams(vmem_limit_bytes=24 << 20),
        name="cross_products",
    )(pairs, bands)


def lag_kernel(valid_ref, cross_ref, table_ref, out_ref):
    i = pl.program_id(0)
    table = table_ref[...].reshape(256, NLAG)
    for p in range(4):
        piece = cross_ref[:, p].reshape(256, BLK)
        part = lax.dot_general(piece, table, (((0,), (0,)), ((), ())), preferred_element_type=jnp.float32)

        @pl.when(i == 0)
        def _():
            out_ref[p] = part

        @pl.when(i > 0)
        def _():
            out_ref[p] += part

    @pl.when(i == pl.num_programs(0) - 1)
    def _():
        for p in range(4):
            out_ref[p] = out_ref[p] * (valid_ref[p].astype(jnp.float32) * (1.0 / math.sqrt(NB)))


def lag_sums(valid, owned, table):
    return pl.pallas_call(
        lag_kernel,
        out_shape=jax.ShapeDtypeStruct((4, BLK, NLAG), jnp.float32),
        grid_spec=pltpu.PrefetchScalarGridSpec(
            num_scalar_prefetch=1,
            grid=(16,),
            in_specs=[
                pl.BlockSpec((8, 4, 2, 16, BLK), lambda i, *_: (i, 0, 0, 0, 0)),
                pl.BlockSpec((8, 2, 16, NLAG), lambda i, *_: (i, 0, 0, 0)),
            ],
            out_specs=pl.BlockSpec((4, BLK, NLAG), lambda i, *_: (0, 0, 0)),
        ),
        compiler_params=pltpu.CompilerParams(vmem_limit_bytes=24 << 20),
        name="lag_sums",
    )(valid, owned, table)


def body(samples, fan_taps, pair_blocks, pair_valid, coil_offsets):
    x = samples.reshape(BLK, NT)
    before = lax.ppermute(x[BLK - HALF :], AXES, [(i, i + 1) for i in range(NDEV - 1)])
    after = lax.ppermute(x[:HALF], AXES, [(i + 1, i) for i in range(NDEV - 1)])
    wide = jnp.concatenate([before, x, after], axis=0)
    by_residue = fan_taps.reshape(TAPS, 64, 32).transpose(2, 0, 1)
    low, high = by_residue[:QT], jnp.concatenate([by_residue[QT : QT + 1], by_residue[:QT:-1]], axis=0)
    taps = jnp.concatenate([low, high], axis=2)
    white = whiten_block(wide, jnp.asarray(second_stage_table()), taps, coil_offsets)
    bands = lax.all_to_all(white, AXES, split_axis=0, concat_axis=0, tiled=True)
    cross = cross_products(pair_blocks.reshape(-1), bands)
    owned = lax.all_to_all(cross.reshape(NDEV, 4, 2, 16, BLK), AXES, split_axis=0, concat_axis=0, tiled=True)
    return lag_sums(pair_valid, owned, jnp.asarray(inverse_table()))


def solution(mesh):
    return jax.shard_map(
        body,
        mesh=mesh,
        in_specs=(P(AXES, None, None), P(), P(), P(AXES), P()),
        out_specs=P(AXES, None, None),
        check_vma=False,
    )
```

time: 237 us -> 148 us (0.62)
  other arithmetic: 101 us -> 1.57 us
  blocking collectives: 0 us -> 57.4 us
  Pallas kernels: 0 us -> 44.5 us
  waiting for transfers between devices: 53.4 us -> 21.4 us
  local copies, waits for them, and re-layouts: 31.9 us -> 3.84 us
  matrix products: 26.3 us -> 0 us
  starting transfers between devices: 23.9 us -> 18.8 us
    all_to_all x0 -> x1, blocking collectives: none -> 57.4 us  [body(): lax.all_to_all(cross.reshape(NDEV, 4, 2, 16, BLK), AXES, split_axis=0, co...]
    pallas_call x0 -> x3, Pallas kernels: none -> 44.5 us  [the longest x1 16.6 us: lag_sums(): pl.pallas_call(lag_kernel, out_shape=jax.ShapeDtypeStruct((4, BLK, NLAG),...]
    add x3 -> x0, other arithmetic: 40.1 us -> none  [the longest x1 40 us: whiten(): filtered + fan_taps[offset][None, None, :, None] * padded[:, :, :, offset...]
    all_to_all x2 -> x1, waiting for transfers between devices: 53.4 us -> 18.7 us  [body(): bands = lax.all_to_all(white, AXES, split_axis=0, concat_axis=0, tiled=True)]
    dot_general x2 -> x0, matrix products: 26.3 us -> none  [the longest x1 22.9 us: body(): jnp.einsum('cst,tk->skc', samples, forward, preferred_element_type=jnp.fl...]
    another operation x7 -> x0, other arithmetic: 24.7 us -> none
    sub x3 -> x0, other arithmetic: 22 us -> none  [the longest x1 22 us: forward_tables(): cosine = (cos_a * cos_b - sin_a * sin_b).reshape(length, bin_count)]
    convert_element_type x1 -> x0, local copies, waits for them, and re-layouts: 9.46 us -> none  [whiten(): (filtered * lax.rsqrt(mean_power + EPSILON)[:, None]).astype(jnp.bfloat16)]
  transfers between devices with their start and end apart: 4 -> 3, of which waited for: 2 -> 2; matrix products, arithmetic and copies ran while one was open for 10% -> 2% of each run, Pallas kernels for 0% -> 0%
where the time goes in v1:
time: 148 us
  blocking collectives  57.4 us (39%)
  Pallas kernels  44.5 us (30%)
  waiting for transfers between devices  21.4 us (14%)
  starting transfers between devices  18.8 us (13%)
  local copies, waits for them, and re-layouts  3.84 us (3%)
  other arithmetic  1.57 us (1%)
    all_to_all x1, blocking collectives, body(): lax.all_to_all(cross.reshape(NDEV, 4, 2, 16, BLK), AXES, split_axis=0, co...  57.4 us
    all_to_all x1, waiting for transfers between devices, body(): bands = lax.all_to_all(white, AXES, split_axis=0, concat_axis=0, tiled=True)  18.7 us
    pallas_call x1, Pallas kernels, lag_sums(): pl.pallas_call(lag_kernel, out_shape=jax.ShapeDtypeStruct((4, BLK, NLAG),...  16.6 us
    pallas_call x1, Pallas kernels, whiten_block(): pl.pallas_call(white_kernel, out_shape=jax.ShapeDtypeStruct((NDEV, 2, 16,...  14.9 us
    pallas_call x1, Pallas kernels, cross_products(): pl.pallas_call(functools.partial(cross_kernel, step), out_shape=jax.Shape...  13 us
    all_to_all x1, starting transfers between devices, body(): bands = lax.all_to_all(white, AXES, split_axis=0, concat_axis=0, tiled=True)  12.3 us
    ppermute x1, starting transfers between devices, body(): lax.ppermute(x[BLK - HALF:], AXES, [(i, i + 1) for i in range(NDEV - 1)])  4.58 us
  transfers between devices with their start and end apart: 3, of which 2 were waited for; matrix products, arithmetic and copies ran while one was open for 2% of the time, Pallas kernels for 0%

profile of v1, /device:TPU:1, one launch (start us, length us, event | category | flops | bytes accessed | tf_op | source)
XLA Modules:
  0.0 147.6 jit_solution(3764499932623049351)
XLA Ops:
  0.0 1.7 %slice_bitcast_fusion.1 = (bf16[16,4096]{1,0:T(8,128)(2,1)}, bf16[16,4096]{1,0:T(8,128)(2,1)}) fusion(bf16[128,1,4096]{2,0,1:T(8,128)(2,1)} %param.7), kind=kLoop, calls=%fused_computation.3 | loop fusion | bytes 524288 | tf_op jit(solution)/shard_map/slice | solution.py:278
  1.7 4.6 %collective-permute-start = (bf16[16,4096]{1,0:T(8,128)(2,1)}, bf16[16,4096]{1,0:T(8,128)(2,1)S(1)}, u32[]{:S(2)}, u32[]{:S(2)}) collective-permute-start(bf16[16,4096]{1,0:T(8,128)(2,1)} %get-tuple-element.5), channel_id=1, source_target_pairs={{0,1},{1,2},{2,3},{3,4},{4,5},{5,6},{6,7},{7,8},{8,9},{9,10},{10,1... | collective-permute-start | bytes 393224 | tf_op jit(solution)/shard_map/ppermute | solution.py:278
  6.3 1.9 %collective-permute-start.1 = (bf16[16,4096]{1,0:T(8,128)(2,1)}, bf16[16,4096]{1,0:T(8,128)(2,1)}, u32[]{:S(2)}, u32[]{:S(2)}) collective-permute-start(bf16[16,4096]{1,0:T(8,128)(2,1)} %get-tuple-element.6), channel_id=1, source_target_pairs={{1,0},{2,1},{3,2},{4,3},{5,4},{6,5},{7,6},{8,7},{9,8},{10,9},{11,1... | collective-permute-start | bytes 393224 | tf_op jit(solution)/shard_map/ppermute | solution.py:279
  8.2 1.3 reshape.16
  9.5 0.4 copy.9
  10.0 0.0 copy-start.1
  10.0 0.0 copy-start.2
  10.1 0.2 maximum_maximum_fusion.taps_ref
  10.2 0.0 collective-permute-done
  10.3 2.6 %collective-permute-done.1 = bf16[16,4096]{1,0:T(8,128)(2,1)} collective-permute-done((bf16[16,4096]{1,0:T(8,128)(2,1)}, bf16[16,4096]{1,0:T(8,128)(2,1)}, u32[]{:S(2)}, u32[]{:S(2)}) %collective-permute-start.1) | collective-permute-done | bytes 131104 | tf_op jit(solution)/shard_map/ppermute | solution.py:279
  12.9 1.4 pad_maximum_fusion.x_ref
  14.3 0.0 copy-done.1
  14.3 0.0 copy-done.2
  14.3 0.0 copy-start.4
  14.3 14.9 %whiten_block.1 = bf16[128,2,16,128]{3,2,1,0:T(8,128)(2,1)} custom-call(bf16[160,4096]{1,0:T(8,128)(2,1)S(1)} %pad_maximum_fusion.x_ref, bf16[16,256,256]{2,1,0:T(8,128)(2,1)S(1)} %copy-done.1, f32[16,33,128]{2,1,0:T(8,128)S(1)} %maximum_maximum_fusion.taps_ref, s32[128]{0:T(128)S(1)} %copy-done.2), custom_call_target="tpu_custom_call" | custom-call | tf_op jit(solution)/shard_map/whiten_block/pallas_call | solution.py:177
  29.3 12.3 %all-to-all-start = ((bf16[128,2,16,128]{3,2,1,0:T(8,128)(2,1)}), bf16[128,2,16,128]{3,2,1,0:T(8,128)(2,1)S(1)}, u32[]{:S(2)}, u32[]{:S(2)}) async-start(bf16[128,2,16,128]{3,2,1,0:T(8,128)(2,1)} %whiten_block.1), calls=%async_computation | async-start | bytes 2097152 | tf_op jit(solution)/shard_map/all_to_all | solution.py:285
  41.6 0.0 copy-done.4
  41.6 0.1 copy.8
  41.7 0.2 reshape.14.pairs_ref
  41.9 18.7 %all-to-all-done.bands_ref = bf16[128,2,16,128]{3,2,1,0:T(8,128)(2,1)S(1)} async-done(((bf16[128,2,16,128]{3,2,1,0:T(8,128)(2,1)}), bf16[128,2,16,128]{3,2,1,0:T(8,128)(2,1)S(1)}, u32[]{:S(2)}, u32[]{:S(2)}) %all-to-all-start) | async-done | bytes 1048608 | tf_op jit(solution)/shard_map/all_to_all | solution.py:285
  60.6 13.0 %cross_products.1 = bf16[512,2,16,128]{3,2,1,0:T(8,128)(2,1)S(1)} custom-call(s32[1024]{0:T(1024)S(1)} %reshape.14.pairs_ref, bf16[128,2,16,128]{3,2,1,0:T(8,128)(2,1)S(1)} %all-to-all-done.bands_ref), custom_call_target="tpu_custom_call" | custom-call | tf_op jit(solution)/shard_map/cross_products/pallas_call | solution.py:222
  73.6 0.0 copy-start
  73.6 0.0 copy-start.3
  73.7 57.4 %all_to_all.10.cross_ref = bf16[128,4,2,16,128]{4,3,2,1,0:T(8,128)(2,1)S(1)} all-to-all(bf16[128,4,2,16,128]{4,3,2,1,0:T(8,128)(2,1)S(1)} %bitcast.7), channel_id=1, replica_groups=mesh['group'=4,'shard'=32] {'group','shard'}, dimensions={0} | all-to-all | bytes 8388608 | tf_op jit(solution)/shard_map/all_to_all | solution.py:287
  131.0 0.0 copy-done
  131.0 0.0 copy-done.3
  131.0 16.6 %lag_sums.1 = f32[4,128,512]{2,1,0:T(8,128)} custom-call(s32[4]{0:T(128)S(1)} %copy-done.3, bf16[128,4,2,16,128]{4,3,2,1,0:T(8,128)(2,1)S(1)} %all_to_all.10.cross_ref, bf16[128,2,16,512]{3,2,1,0:T(8,128)(2,1)S(1)} %copy-done), custom_call_target="tpu_custom_call" | custom-call | tf_op jit(solution)/shard_map/lag_sums/pallas_call | solution.py:259
  (4 shorter events, 0.1 us)
Async XLA Ops:
  1.7 8.6 %collective-permute-start = (bf16[16,4096]{1,0:T(8,128)(2,1)}, bf16[16,4096]{1,0:T(8,128)(2,1)S(1)}, u32[]{:S(2)}, u32[]{:S(2)}) collective-permute-start(bf16[16,4096]{1,0:T(8,128)(2,1)} %get-tuple-element.5), channel_id=1, source_target_pairs={{0,1},{1,2},{2,3},{3,4},{4,5},{5,6},{6,7},{7,8},{8,9},{9,10},{10,1... | collective-permute-start | bytes 393224 | tf_op jit(solution)/shard_map/ppermute | solution.py:278
  6.3 6.6 %collective-permute-start.1 = (bf16[16,4096]{1,0:T(8,128)(2,1)}, bf16[16,4096]{1,0:T(8,128)(2,1)}, u32[]{:S(2)}, u32[]{:S(2)}) collective-permute-start(bf16[16,4096]{1,0:T(8,128)(2,1)} %get-tuple-element.6), channel_id=1, source_target_pairs={{1,0},{2,1},{3,2},{4,3},{5,4},{6,5},{7,6},{8,7},{9,8},{10,9},{11,1... | collective-permute-start | bytes 393224 | tf_op jit(solution)/shard_map/ppermute | solution.py:279
  10.0 4.3 %copy-start.1 = (bf16[16,256,256]{2,1,0:T(8,128)(2,1)S(1)}, bf16[16,256,256]{2,1,0:T(8,128)(2,1)}, u32[]{:S(2)}) copy-start(bf16[16,256,256]{2,1,0:T(8,128)(2,1)} %constant.4.clone.table_ref) | copy-start | bytes 6291460
  10.0 4.3 %copy-start.2 = (s32[128]{0:T(128)S(1)}, s32[128]{0:T(128)}, u32[]{:S(2)}) copy-start(s32[128]{0:T(128)} %offsets_ref.1) | copy-start | bytes 1540
  14.3 27.3 %copy-start.4 = (s32[512,2]{0,1:T(2,128)S(1)}, s32[512,2]{0,1:T(2,128)}, u32[]{:S(2)}) copy-start(s32[512,2]{0,1:T(2,128)} %param.9) | copy-start | bytes 12292
  29.3 31.4 %all-to-all-start = ((bf16[128,2,16,128]{3,2,1,0:T(8,128)(2,1)}), bf16[128,2,16,128]{3,2,1,0:T(8,128)(2,1)S(1)}, u32[]{:S(2)}, u32[]{:S(2)}) async-start(bf16[128,2,16,128]{3,2,1,0:T(8,128)(2,1)} %whiten_block.1), calls=%async_computation | async-start | bytes 2097152 | tf_op jit(solution)/shard_map/all_to_all | solution.py:285
  73.6 57.4 %copy-start = (bf16[128,2,16,512]{3,2,1,0:T(8,128)(2,1)S(1)}, bf16[128,2,16,512]{3,2,1,0:T(8,128)(2,1)}, u32[]{:S(2)}) copy-start(bf16[128,2,16,512]{3,2,1,0:T(8,128)(2,1)} %constant.5.clone.table_ref) | copy-start | bytes 12582916
  73.6 57.4 %copy-start.3 = (s32[4]{0:T(128)S(1)}, s32[4]{0:T(128)}, u32[]{:S(2)}) copy-start(s32[4]{0:T(128)} %valid_ref.1) | copy-start | bytes 52

commit v2 on v1

--- a/solution.py
+++ b/solution.py
@@ -1,4 +1,3 @@
-import functools
 import math
 
 import jax
@@ -19,6 +18,7 @@
 EPSILON = 1e-05
 AXES = ("group", "shard")
 NDEV = 128
+MESH = pl.DeviceIdType.MESH
 TAPS = 2 * HALF + 1
 QT = 16
 
@@ -52,13 +52,6 @@
     table[0, 1, :, 0, 64:] = cos[0, :, 64:]
     table[0, 1, :, 1, 64:] = -sin[0, :, 64:]
     return (table.reshape(QT, 256, 256) / math.sqrt(NT)).astype(ml_dtypes.bfloat16)
-
-
-def inverse_table():
-    bins = tile_bins().reshape(NDEV, 16)
-    lags = np.arange(NLAG) - NLAG // 2
-    phase = 2 * np.pi * ((bins[:, :, None] * lags) % NT) / NT
-    return np.stack([np.cos(phase), -np.sin(phase)], axis=1).astype(ml_dtypes.bfloat16)
 
 
 def real_fft(rows):
@@ -196,81 +189,186 @@
     )(wide, table, taps, offsets)
 
 
-def cross_kernel(step, pairs_ref, bands_ref, out_ref, rolled_ref):
-    i = pl.program_id(0)
-
-    @pl.when(i == 0)
-    def _():
-        @pl.loop(0, NDEV)
-        def _(block):
-            both = bands_ref[block].astype(jnp.float32).reshape(32, 128)
-            rolled_ref[block] = pltpu.roll(both, 64, 1).astype(jnp.bfloat16).reshape(2, 16, 128)
-
-    @pl.loop(0, step, unroll=4)
-    def _(p):
-        a = pairs_ref[2 * (i * step + p)]
-        b = pairs_ref[2 * (i * step + p) + 1]
-        left = bands_ref[a].astype(jnp.float32)
-        right = rolled_ref[b].astype(jnp.float32)
-        out_ref[p, 0] = (left[0] * right[0] + left[1] * right[1]).astype(jnp.bfloat16)
-        out_ref[p, 1] = (left[1] * right[0] - left[0] * right[1]).astype(jnp.bfloat16)
-
-
-def cross_products(pairs, bands):
-    count = pairs.shape[0] // 2
-    step = count // 8
+def offsets_of(i):
+    return i % 4, (i // 4 + 2 * i) % 4, (i // 16 + 3 * i) % 4, i // 64
+
+
+def place():
+    shard = lax.axis_index("shard")
+    return lax.axis_index("group"), shard // 8, (shard // 2) % 4, shard % 2
+
+
+def partner(i, back):
+    x, z, y, core = place()
+    dx, dz, dy, dc = offsets_of(i)
+    other = (core + dc) % 2
+    sign = 2 * other - 1 if back else 1 - 2 * core
+    return (x + 4 + sign * dx) % 4, ((z + 4 + sign * dz) % 4 * 4 + (y + 4 + sign * dy) % 4) * 2 + other
+
+
+def signal_everyone(barrier):
+    x, z, y, core = place()
+
+    @pl.loop(0, 16)
+    def _(i):
+        there = (x + i // 4) % 4
+        row = (z + i % 4) % 4 * 8
+        for dy in range(4):
+            for dc in range(2):
+                shard = row + (y + dy) % 4 * 2 + (core + dc) % 2
+
+                def signal():
+                    pl.semaphore_signal(barrier, inc=1, device_id=(there, shard), device_id_type=MESH)
+
+                if dy == 0 and dc == 0:
+                    pl.when(i > 0)(signal)
+                else:
+                    signal()
+
+
+def lag_rows(i, coarse_ref, fine_ref, table_ref):
+    group, shard = partner(i, True)
+    band = group * 32 + shard
+    tile, part = band // 8, band % 8
+    residue = jnp.where(part < 4, tile, jnp.where(tile == 0, 16, 32 - tile))
+    cos_a, sin_a = coarse_ref[0, pl.ds(residue, 1), :], coarse_ref[1, pl.ds(residue, 1), :]
+    rows = pl.ds(pl.multiple_of(part % 4 * 16, 16), 16)
+    cos_b, sin_b = fine_ref[0, rows, :], fine_ref[1, rows, :]
+    table_ref[i, 0] = (cos_a * cos_b - sin_a * sin_b).astype(jnp.bfloat16)
+    table_ref[i, 1] = (-(sin_a * cos_b + cos_a * sin_b)).astype(jnp.bfloat16)
+
+
+def pair_kernel(
+    pairs_ref, white_ref, out_ref, bands_ref, rolled_ref, send_ref, recv_ref, table_ref,
+    coarse_ref, fine_ref, band_send, band_recv, cross_send, cross_recv,
+):
+    me = lax.axis_index("group") * 32 + lax.axis_index("shard")
+    barrier = pltpu.get_barrier_semaphore()
+    signal_everyone(barrier)
+    pl.semaphore_wait(barrier, NDEV - 1)
+
+    @pl.loop(1, NDEV)
+    def _(i):
+        group, shard = partner(i, False)
+        pltpu.make_async_remote_copy(
+            src_ref=white_ref.at[group * 32 + shard],
+            dst_ref=bands_ref.at[me],
+            send_sem=band_send,
+            recv_sem=band_recv,
+            device_id=(group, shard),
+            device_id_type=MESH,
+        ).start()
+
+    bands_ref[me] = white_ref[me]
+    lag = lax.broadcasted_iota(jnp.int32, (64, NLAG), 1) - NLAG // 2
+    row = lax.broadcasted_iota(jnp.int32, (64, NLAG), 0)
+    fine = ((32 * row * lag) & (NT - 1)).astype(jnp.float32) * (2.0 * math.pi / NT)
+    coarse = ((row * lag) & (NT - 1)).astype(jnp.float32) * (2.0 * math.pi / NT)
+    fine_ref[0] = jnp.cos(fine)
+    fine_ref[1] = jnp.sin(fine)
+    coarse_ref[0] = jnp.cos(coarse[:32])
+    coarse_ref[1] = jnp.sin(coarse[:32])
+
+    @pl.loop(0, NDEV)
+    def _(i):
+        lag_rows(i, coarse_ref, fine_ref, table_ref)
+
+    out_ref[...] = jnp.zeros_like(out_ref)
+    everyone = pl.ds(0, NDEV - 1)
+    arrivals = pltpu.make_async_remote_copy(
+        src_ref=white_ref.at[everyone],
+        dst_ref=bands_ref.at[everyone],
+        send_sem=band_send,
+        recv_sem=band_recv,
+        device_id=partner(1, False),
+        device_id_type=MESH,
+    )
+    arrivals.wait()
+
+    @pl.loop(0, NDEV)
+    def _(block):
+        both = bands_ref[block].astype(jnp.float32).reshape(32, 128)
+        rolled_ref[block] = pltpu.roll(both, 64, 1).astype(jnp.bfloat16).reshape(2, 16, 128)
+
+    def products(owner, to_ref, slot):
+        for p in range(4):
+            a = pairs_ref[8 * owner + 2 * p]
+            b = pairs_ref[8 * owner + 2 * p + 1]
+            left = bands_ref[a].astype(jnp.float32)
+            right = rolled_ref[b].astype(jnp.float32)
+            to_ref[slot, p, 0] = (left[0] * right[0] + left[1] * right[1]).astype(jnp.bfloat16)
+            to_ref[slot, p, 1] = (left[1] * right[0] - left[0] * right[1]).astype(jnp.bfloat16)
+
+    @pl.loop(1, NDEV)
+    def _(i):
+        group, shard = partner(i, False)
+        products(group * 32 + shard, send_ref, i)
+        pltpu.make_async_remote_copy(
+            src_ref=send_ref.at[i],
+            dst_ref=recv_ref.at[i],
+            send_sem=cross_send,
+            recv_sem=cross_recv.at[i // 8],
+            device_id=(group, shard),
+            device_id_type=MESH,
+        ).start()
+
+    products(me, recv_ref, 0)
+
+    def accumulate(first, count, piece_of):
+        pltpu.make_async_remote_copy(
+            src_ref=send_ref.at[pl.ds(first, count)],
+            dst_ref=recv_ref.at[pl.ds(first, count)],
+            send_sem=cross_send,
+            recv_sem=cross_recv.at[piece_of],
+            device_id=partner(1, False),
+            device_id_type=MESH,
+        ).wait_recv()
+        slots = pl.ds(piece_of * 8, 8)
+        table = table_ref[slots].reshape(256, NLAG)
+        for p in range(4):
+            piece = recv_ref[slots, p].reshape(256, BLK)
+            out_ref[p] += lax.dot_general(
+                piece, table, (((0,), (0,)), ((), ())), preferred_element_type=jnp.float32
+            )
+
+    accumulate(1, 7, 0)
+
+    @pl.loop(1, 16)
+    def _(g):
+        accumulate(g * 8, 8, g)
+
+    pltpu.make_async_remote_copy(
+        src_ref=send_ref.at[pl.ds(1, NDEV - 1)],
+        dst_ref=recv_ref.at[pl.ds(1, NDEV - 1)],
+        send_sem=cross_send,
+        recv_sem=cross_recv.at[0],
+        device_id=partner(1, False),
+        device_id_type=MESH,
+    ).wait_send()
+
+
+def correlate(pairs, white):
     return pl.pallas_call(
-        functools.partial(cross_kernel, step),
-        out_shape=jax.ShapeDtypeStruct((count, 2, 16, BLK), jnp.bfloat16),
-        grid_spec=pltpu.PrefetchScalarGridSpec(
-            num_scalar_prefetch=1,
-            grid=(8,),
-            in_specs=[pl.BlockSpec((NDEV, 2, 16, BLK), lambda i, *_: (0, 0, 0, 0))],
-            out_specs=pl.BlockSpec((step, 2, 16, BLK), lambda i, *_: (i, 0, 0, 0)),
-            scratch_shapes=[pltpu.VMEM((NDEV, 2, 16, BLK), jnp.bfloat16)],
-        ),
-        compiler_params=pltpu.CompilerParams(vmem_limit_bytes=24 << 20),
-        name="cross_products",
-    )(pairs, bands)
-
-
-def lag_kernel(valid_ref, cross_ref, table_ref, out_ref):
-    i = pl.program_id(0)
-    table = table_ref[...].reshape(256, NLAG)
-    for p in range(4):
-        piece = cross_ref[:, p].reshape(256, BLK)
-        part = lax.dot_general(piece, table, (((0,), (0,)), ((), ())), preferred_element_type=jnp.float32)
-
-        @pl.when(i == 0)
-        def _():
-            out_ref[p] = part
-
-        @pl.when(i > 0)
-        def _():
-            out_ref[p] += part
-
-    @pl.when(i == pl.num_programs(0) - 1)
-    def _():
-        for p in range(4):
-            out_ref[p] = out_ref[p] * (valid_ref[p].astype(jnp.float32) * (1.0 / math.sqrt(NB)))
-
-
-def lag_sums(valid, owned, table):
-    return pl.pallas_call(
-        lag_kernel,
+        pair_kernel,
         out_shape=jax.ShapeDtypeStruct((4, BLK, NLAG), jnp.float32),
-        grid_spec=pltpu.PrefetchScalarGridSpec(
-            num_scalar_prefetch=1,
-            grid=(16,),
-            in_specs=[
-                pl.BlockSpec((8, 4, 2, 16, BLK), lambda i, *_: (i, 0, 0, 0, 0)),
-                pl.BlockSpec((8, 2, 16, NLAG), lambda i, *_: (i, 0, 0, 0)),
-            ],
-            out_specs=pl.BlockSpec((4, BLK, NLAG), lambda i, *_: (0, 0, 0)),
-        ),
-        compiler_params=pltpu.CompilerParams(vmem_limit_bytes=24 << 20),
-        name="lag_sums",
-    )(valid, owned, table)
+        in_specs=[pl.BlockSpec(memory_space=pltpu.SMEM), pl.BlockSpec(memory_space=pltpu.VMEM)],
+        out_specs=pl.BlockSpec(memory_space=pltpu.VMEM),
+        scratch_shapes=[
+            pltpu.VMEM((NDEV, 2, 16, BLK), jnp.bfloat16),
+            pltpu.VMEM((NDEV, 2, 16, BLK), jnp.bfloat16),
+            pltpu.VMEM((NDEV, 4, 2, 16, BLK), jnp.bfloat16),
+            pltpu.VMEM((NDEV, 4, 2, 16, BLK), jnp.bfloat16),
+            pltpu.VMEM((NDEV, 2, 16, NLAG), jnp.bfloat16),
+            pltpu.VMEM((2, 32, NLAG), jnp.float32),
+            pltpu.VMEM((2, 64, NLAG), jnp.float32),
+            pltpu.SemaphoreType.DMA,
+            pltpu.SemaphoreType.DMA,
+            pltpu.SemaphoreType.DMA,
+            pltpu.SemaphoreType.DMA((16,)),
+        ],
+        compiler_params=pltpu.CompilerParams(collective_id=0, has_side_effects=True, vmem_limit_bytes=40 << 20),
+        name="correlate",
+    )(pairs, white)
 
 
 def body(samples, fan_taps, pair_blocks, pair_valid, coil_offsets):
@@ -282,10 +380,9 @@
     low, high = by_residue[:QT], jnp.concatenate([by_residue[QT : QT + 1], by_residue[:QT:-1]], axis=0)
     taps = jnp.concatenate([low, high], axis=2)
     white = whiten_block(wide, jnp.asarray(second_stage_table()), taps, coil_offsets)
-    bands = lax.all_to_all(white, AXES, split_axis=0, concat_axis=0, tiled=True)
-    cross = cross_products(pair_blocks.reshape(-1), bands)
-    owned = lax.all_to_all(cross.reshape(NDEV, 4, 2, 16, BLK), AXES, split_axis=0, concat_axis=0, tiled=True)
-    return lag_sums(pair_valid, owned, jnp.asarray(inverse_table()))
+    sums = correlate(pair_blocks.reshape(-1), white)
+    weights = pair_valid.astype(jnp.float32) * (1.0 / math.sqrt(NB))
+    return sums * weights[:, None, None]
 
 
 def solution(mesh):

time: 148 us -> 118 us (0.80)
  blocking collectives: 57.4 us -> 0 us
  Pallas kernels: 44.5 us -> 101 us
  waiting for transfers between devices: 21.4 us -> 0.01 us
  starting transfers between devices: 18.8 us -> 6.51 us
  other arithmetic: 1.57 us -> 4 us
  local copies, waits for them, and re-layouts: 3.84 us -> 6.2 us
    all_to_all x1 -> x0, blocking collectives: 57.4 us -> none  [body(): lax.all_to_all(cross.reshape(NDEV, 4, 2, 16, BLK), AXES, split_axis=0, co...]
    pallas_call x2 -> x1, Pallas kernels: 29.6 us -> 86.7 us  [correlate(): pl.pallas_call(pair_kernel, out_shape=jax.ShapeDtypeStruct((4, BLK, NLAG)...]
    all_to_all x1 -> x0, waiting for transfers between devices: 18.7 us -> none  [body(): bands = lax.all_to_all(white, AXES, split_axis=0, concat_axis=0, tiled=True)]
    all_to_all x1 -> x0, starting transfers between devices: 12.3 us -> none  [body(): bands = lax.all_to_all(white, AXES, split_axis=0, concat_axis=0, tiled=True)]
    ppermute x1, waiting for transfers between devices: 2.61 us -> 0.01 us  [body(): after = lax.ppermute(x[:HALF], AXES, [(i + 1, i) for i in range(NDEV - 1)])]
    mul x0 -> x2, other arithmetic: none -> 1.82 us  [the longest x1 1.16 us: body(): return sums * weights[:, None, None]]
  transfers between devices with their start and end apart: 3 -> 2, of which waited for: 2 -> 0; matrix products, arithmetic and copies ran while one was open for 2% -> 5% of each run, Pallas kernels for 0% -> 0%
where the time goes in v2:
time: 118 us
  Pallas kernels  101 us (86%)
  starting transfers between devices  6.51 us (6%)
  local copies, waits for them, and re-layouts  6.2 us (5%)
  other arithmetic  4 us (3%)
    pallas_call x1, Pallas kernels, correlate(): pl.pallas_call(pair_kernel, out_shape=jax.ShapeDtypeStruct((4, BLK, NLAG)...  86.7 us
    pallas_call x1, Pallas kernels, whiten_block(): pl.pallas_call(white_kernel, out_shape=jax.ShapeDtypeStruct((NDEV, 2, 16,...  14 us
    ppermute x1, starting transfers between devices, body(): lax.ppermute(x[BLK - HALF:], AXES, [(i, i + 1) for i in range(NDEV - 1)])  4.58 us
  transfers between devices with their start and end apart: 2, of which 0 were waited for; matrix products, arithmetic and copies ran while one was open for 5% of the time, Pallas kernels for 0%

profile of v2, /device:TPU:1, one launch (start us, length us, event | category | flops | bytes accessed | tf_op | source)
XLA Modules:
  0.0 117.5 jit_solution(9998268319422326485)
XLA Ops:
  0.0 1.7 %slice_bitcast_fusion.1 = (bf16[16,4096]{1,0:T(8,128)(2,1)}, bf16[16,4096]{1,0:T(8,128)(2,1)}) fusion(bf16[128,1,4096]{2,0,1:T(8,128)(2,1)} %param.6), kind=kLoop, calls=%fused_computation.4 | loop fusion | bytes 524288 | tf_op jit(solution)/shard_map/slice | solution.py:376
  1.7 4.6 %collective-permute-start = (bf16[16,4096]{1,0:T(8,128)(2,1)}, bf16[16,4096]{1,0:T(8,128)(2,1)}, u32[]{:S(2)}, u32[]{:S(2)}) collective-permute-start(bf16[16,4096]{1,0:T(8,128)(2,1)} %get-tuple-element.5), channel_id=1, source_target_pairs={{0,1},{1,2},{2,3},{3,4},{4,5},{5,6},{6,7},{7,8},{8,9},{9,10},{10,1... | collective-permute-start | bytes 393224 | tf_op jit(solution)/shard_map/ppermute | solution.py:376
  6.3 1.9 %collective-permute-start.1 = (bf16[16,4096]{1,0:T(8,128)(2,1)}, bf16[16,4096]{1,0:T(8,128)(2,1)}, u32[]{:S(2)}, u32[]{:S(2)}) collective-permute-start(bf16[16,4096]{1,0:T(8,128)(2,1)} %get-tuple-element.6), channel_id=1, source_target_pairs={{1,0},{2,1},{3,2},{4,3},{5,4},{6,5},{7,6},{8,7},{9,8},{10,9},{11,1... | collective-permute-start | bytes 393224 | tf_op jit(solution)/shard_map/ppermute | solution.py:377
  8.2 0.7 convert_multiply_fusion
  8.9 1.3 %reshape.14 = f32[33,64,32]{2,1,0:T(8,128)S(1)} reshape(f32[33,2048]{1,0:T(8,128)} %param.7) | data formatting | bytes 540672 | tf_op jit(solution)/shard_map/reshape | solution.py:379
  10.2 0.0 copy-start.3
  10.2 0.4 copy.8
  10.6 0.0 copy-start.2
  10.7 0.7 rev.3
  11.5 0.0 copy-done.3
  11.5 0.0 copy-start
  11.5 0.0 copy-start.1
  11.5 0.9 copy.7
  12.3 1.1 reshape.12.pairs_ref
  13.4 1.1 maximum_maximum_fusion.taps_ref
  14.6 0.0 collective-permute-done
  14.6 0.0 collective-permute-done.1
  14.6 0.0 copy-done.2
  14.6 1.1 pad_maximum_fusion.x_ref
  15.7 0.0 copy-done
  15.7 0.0 copy-done.1
  15.7 14.0 %whiten_block.1.white_ref = bf16[128,2,16,128]{3,2,1,0:T(8,128)(2,1)S(1)} custom-call(bf16[160,4096]{1,0:T(8,128)(2,1)S(1)} %pad_maximum_fusion.x_ref, bf16[16,256,256]{2,1,0:T(8,128)(2,1)S(1)} %copy-done, f32[16,33,128]{2,1,0:T(8,128)S(1)} %maximum_maximum_fusion.taps_ref, s32[128]{0:T(128)S(1)} %copy-done.1), custom_call_target="tpu_custom_call" | custom-call | tf_op jit(solution)/shard_map/whiten_block/pallas_call | solution.py:170
  29.7 86.7 %correlate.1 = f32[4,128,512]{2,1,0:T(8,128)S(1)} custom-call(s32[1024]{0:T(1024)S(1)} %reshape.12.pairs_ref, bf16[128,2,16,128]{3,2,1,0:T(8,128)(2,1)S(1)} %whiten_block.1.white_ref), custom_call_target="tpu_custom_call" | custom-call | tf_op jit(solution)/shard_map/correlate/pallas_call | solution.py:351
  116.4 1.2 broadcast_multiply_fusion
  (3 shorter events, 0.0 us)
Async XLA Ops:
  1.7 12.9 %collective-permute-start = (bf16[16,4096]{1,0:T(8,128)(2,1)}, bf16[16,4096]{1,0:T(8,128)(2,1)}, u32[]{:S(2)}, u32[]{:S(2)}) collective-permute-start(bf16[16,4096]{1,0:T(8,128)(2,1)} %get-tuple-element.5), channel_id=1, source_target_pairs={{0,1},{1,2},{2,3},{3,4},{4,5},{5,6},{6,7},{7,8},{8,9},{9,10},{10,1... | collective-permute-start | bytes 393224 | tf_op jit(solution)/shard_map/ppermute | solution.py:376
  6.3 8.3 %collective-permute-start.1 = (bf16[16,4096]{1,0:T(8,128)(2,1)}, bf16[16,4096]{1,0:T(8,128)(2,1)}, u32[]{:S(2)}, u32[]{:S(2)}) collective-permute-start(bf16[16,4096]{1,0:T(8,128)(2,1)} %get-tuple-element.6), channel_id=1, source_target_pairs={{1,0},{2,1},{3,2},{4,3},{5,4},{6,5},{7,6},{8,7},{9,8},{10,9},{11,1... | collective-permute-start | bytes 393224 | tf_op jit(solution)/shard_map/ppermute | solution.py:377
  10.2 1.3 %copy-start.3 = (s32[512,2]{0,1:T(2,128)S(1)}, s32[512,2]{0,1:T(2,128)}, u32[]{:S(2)}) copy-start(s32[512,2]{0,1:T(2,128)} %param.8) | copy-start | bytes 12292
  10.6 4.0 %copy-start.2 = (bf16[128,1,4096]{2,0,1:T(8,128)(2,1)S(1)}, bf16[128,1,4096]{2,0,1:T(8,128)(2,1)}, u32[]{:S(2)}) copy-start(bf16[128,1,4096]{2,0,1:T(8,128)(2,1)} %param.6) | copy-start | bytes 3145732
  11.5 4.2 %copy-start = (bf16[16,256,256]{2,1,0:T(8,128)(2,1)S(1)}, bf16[16,256,256]{2,1,0:T(8,128)(2,1)}, u32[]{:S(2)}) copy-start(bf16[16,256,256]{2,1,0:T(8,128)(2,1)} %constant.4.clone.table_ref) | copy-start | bytes 6291460
  11.5 4.2 %copy-start.1 = (s32[128]{0:T(128)S(1)}, s32[128]{0:T(128)}, u32[]{:S(2)}) copy-start(s32[128]{0:T(128)} %offsets_ref.1) | copy-start | bytes 1540

commit v3 on v1

v3 whole, which is shorter than its diff:
```python
import math

import jax
import jax.numpy as jnp
import ml_dtypes
import numpy as np
from jax import lax
from jax.experimental import pallas as pl
from jax.experimental.pallas import tpu as pltpu
from jax.sharding import PartitionSpec as P

HALF = 16
NLAG = 512
NT = 4096
NB = 2048
BLK = 128
WIDE = BLK + 2 * HALF
EPSILON = 1e-05
AXES = ("group", "shard")
NDEV = 128
MESH = pl.DeviceIdType.MESH
TAPS = 2 * HALF + 1
QT = 16


def residues():
    low = np.arange(QT)
    high = np.where(low == 0, 16, 32 - low)
    return low, high


def tile_bins():
    low, high = residues()
    k2 = np.arange(64)
    return np.concatenate([low[:, None] + 32 * k2, high[:, None] + 32 * k2], axis=1)


def second_stage_table():
    bins = tile_bins()
    b = np.arange(128)
    phase = 2 * np.pi * ((b[None, :, None] * bins[:, None, :]) % NT) / NT
    cos, sin = np.cos(phase), np.sin(phase)
    table = np.zeros((QT, 2, 128, 2, 128))
    conj = np.concatenate([np.ones(64), -np.ones(64)])
    table[:, 0, :, 0] = cos
    table[:, 1, :, 0] = sin * conj
    table[:, 0, :, 1] = -sin
    table[:, 1, :, 1] = cos * conj
    table[0] = 0.0
    table[0, 0, :, 0, :64] = cos[0, :, :64]
    table[0, 0, :, 1, :64] = -sin[0, :, :64]
    table[0, 1, :, 0, 64:] = cos[0, :, 64:]
    table[0, 1, :, 1, 64:] = -sin[0, :, 64:]
    return (table.reshape(QT, 256, 256) / math.sqrt(NT)).astype(ml_dtypes.bfloat16)


def real_fft(rows):
    count = len(rows)
    if count == 2:
        return [(rows[0] + rows[1], None), (rows[0] - rows[1], None)]
    even = real_fft(rows[0::2])
    odd = real_fft(rows[1::2])
    half, quarter = count // 2, count // 4
    out = [None] * (half + 1)
    out[0] = (even[0][0] + odd[0][0], None)
    out[half] = (even[0][0] - odd[0][0], None)
    out[quarter] = (even[quarter][0], -odd[quarter][0])
    for k in range(1, quarter):
        wr, wi = math.cos(2 * math.pi * k / count), -math.sin(2 * math.pi * k / count)
        o_re, o_im = odd[k]
        e_re, e_im = even[k]
        t_re = o_re * wr - o_im * wi
        t_im = o_re * wi + o_im * wr
        out[k] = (e_re + t_re, e_im + t_im)
        out[half - k] = (e_re - t_re, t_im - e_im)
    return out


def offsets_of(i):
    return i % 4, (i // 4 + 2 * i) % 4, (i // 16 + 3 * i) % 4, i // 64


def place():
    shard = lax.axis_index("shard")
    return lax.axis_index("group"), shard // 8, (shard // 2) % 4, shard % 2


def partner(i, back):
    x, z, y, core = place()
    dx, dz, dy, dc = offsets_of(i)
    other = (core + dc) % 2
    sign = 2 * other - 1 if back else 1 - 2 * core
    return (x + 4 + sign * dx) % 4, ((z + 4 + sign * dz) % 4 * 4 + (y + 4 + sign * dy) % 4) * 2 + other


def signal_some(barrier, i):
    x, z, y, core = place()
    there = (x + i // 4) % 4
    row = (z + i % 4) % 4 * 8
    for dy in range(4):
        for dc in range(2):
            shard = row + (y + dy) % 4 * 2 + (core + dc) % 2

            def signal():
                pl.semaphore_signal(barrier, inc=1, device_id=(there, shard), device_id_type=MESH)

            if dy == 0 and dc == 0:
                pl.when(i > 0)(signal)
            else:
                signal()


def first_stage(rows, y_ref, at):
    freq = real_fft(rows)
    for q in range(QT):
        second = freq[16][0] if q == 0 else freq[q][1]
        y_ref[q, at, 0:128] = freq[q][0].astype(jnp.bfloat16)
        y_ref[q, at, 128:256] = second.astype(jnp.bfloat16)


def sort_taps(fan_ref, turned_ref, taps_ref):
    blank = jnp.zeros((128 - TAPS, 128), jnp.float32)

    @pl.loop(0, QT)
    def _(j):
        at = pl.ds(pl.multiple_of(j * 128, 128), 128)
        turned_ref[at, :] = jnp.concatenate([fan_ref[:, at], blank], axis=0).T

    @pl.loop(0, QT)
    def _(q):
        high = jnp.where(q == 0, 16, 32 - q)
        both = jnp.concatenate(
            [turned_ref[pl.ds(q, 64, stride=32), :], turned_ref[pl.ds(high, 64, stride=32), :]], axis=0
        )
        taps_ref[q] = both.T[:40]


def lag_tables(coarse_ref, fine_ref):
    lag = lax.broadcasted_iota(jnp.int32, (64, NLAG), 1) - NLAG // 2
    row = lax.broadcasted_iota(jnp.int32, (64, NLAG), 0)
    fine = ((32 * row * lag) & (NT - 1)).astype(jnp.float32) * (2.0 * math.pi / NT)
    coarse = ((row * lag) & (NT - 1)).astype(jnp.float32) * (2.0 * math.pi / NT)
    fine_ref[0] = jnp.cos(fine)
    fine_ref[1] = jnp.sin(fine)
    coarse_ref[0] = jnp.cos(coarse[:32])
    coarse_ref[1] = jnp.sin(coarse[:32])


def lag_rows(i, coarse_ref, fine_ref, lags_ref):
    group, shard = partner(i, True)
    band = group * 32 + shard
    tile, part = band // 8, band % 8
    residue = jnp.where(part < 4, tile, jnp.where(tile == 0, 16, 32 - tile))
    cos_a, sin_a = coarse_ref[0, pl.ds(residue, 1), :], coarse_ref[1, pl.ds(residue, 1), :]
    rows = pl.ds(pl.multiple_of(part % 4 * 16, 16), 16)
    cos_b, sin_b = fine_ref[0, rows, :], fine_ref[1, rows, :]
    lags_ref[i, 0] = (cos_a * cos_b - sin_a * sin_b).astype(jnp.bfloat16)
    lags_ref[i, 1] = (-(sin_a * cos_b + cos_a * sin_b)).astype(jnp.bfloat16)


def bin_rows(offset, rows_ref):
    lane = lax.broadcasted_iota(jnp.int32, (QT, 128), 1)
    tile = lax.broadcasted_iota(jnp.int32, (QT, 128), 0)
    residue = jnp.where(lane < 64, tile, jnp.where(tile == 0, 16, 32 - tile))
    bins = residue + 32 * (lane & 63)
    theta = ((bins * offset) & (NT - 1)).astype(jnp.float32) * (2.0 * math.pi / NT)
    rows_ref[0] = jnp.cos(theta)
    rows_ref[1] = jnp.sin(theta)
    count = jnp.minimum(bins + 64, NB - 1) - jnp.maximum(bins - 64, 0) + 1
    rows_ref[2] = 1.0 / count.astype(jnp.float32)


def copy_to(src, dst, send_sem, recv_sem, device):
    return pltpu.make_async_remote_copy(
        src_ref=src, dst_ref=dst, send_sem=send_sem, recv_sem=recv_sem, device_id=device, device_id_type=MESH
    )


def kernel(
    pairs_ref, offsets_ref, x_ref, fan_ref, table_hbm, out_ref,
    table_ref, halo_ref, y_ref, even_ref, odd_ref, turned_ref, taps_ref, filt_ref, upto_ref, run_ref, rows_ref,
    white_ref, bands_ref, send_ref, recv_ref, lags_ref, coarse_ref, fine_ref,
    table_sem, halo_send, halo_recv, band_send, band_recv, cross_send, cross_recv,
):
    x, z, y, core = place()
    me = lax.axis_index("group") * 32 + lax.axis_index("shard")
    barrier = pltpu.get_barrier_semaphore()
    fetch = pltpu.make_async_copy(table_hbm, table_ref, table_sem)
    fetch.start()

    @pl.loop(0, 8)
    def _(chunk):
        signal_some(barrier, 2 * chunk)
        signal_some(barrier, 2 * chunk + 1)
        at = pl.ds(pl.multiple_of(chunk * 16, 16), 16)
        to = pl.ds(pl.multiple_of(chunk * 16 + 16, 16), 16)
        first_stage([x_ref[at, a * 128 : (a + 1) * 128].astype(jnp.float32) for a in range(32)], y_ref, to)

    pl.semaphore_wait(barrier, NDEV - 1)
    after, before = (me + 1) % NDEV, (me + NDEV - 1) % NDEV
    to_after = copy_to(
        x_ref.at[pl.ds(BLK - HALF, HALF)], halo_ref.at[0], halo_send.at[0], halo_recv.at[0],
        (after // 32, after % 32),
    )
    to_before = copy_to(
        x_ref.at[pl.ds(0, HALF)], halo_ref.at[1], halo_send.at[1], halo_recv.at[1],
        (before // 32, before % 32),
    )
    to_after.start()
    to_before.start()

    sort_taps(fan_ref, turned_ref, taps_ref)
    bin_rows(offsets_ref[me], rows_ref)
    lag_tables(coarse_ref, fine_ref)

    @pl.loop(0, NDEV)
    def _(i):
        lag_rows(i, coarse_ref, fine_ref, lags_ref)

    to_after.wait()
    to_before.wait()

    @pl.loop(0, 2)
    def _(side):
        edge = jnp.where(side == 0, me > 0, me < NDEV - 1).astype(jnp.float32)
        to = pl.ds(pl.multiple_of(side * (BLK + HALF), 16), 16)
        first_stage(
            [halo_ref[side, :, a * 128 : (a + 1) * 128].astype(jnp.float32) * edge for a in range(32)], y_ref, to
        )

    fetch.wait()
    lanes = lax.broadcasted_iota(jnp.int32, (BLK, 128), 1)
    low = lanes < 64
    k2 = lanes & 63

    def second_stage(q, to_ref):
        both = jnp.dot(y_ref[q], table_ref[q], preferred_element_type=jnp.float32)
        to_ref[0] = both[:, :128]
        to_ref[1] = both[:, 128:]

    def fan(q, spec_ref):
        for h in (0, 64):
            re = jnp.zeros((64, 128), jnp.float32)
            im = re
            for t in range(TAPS):
                tap = taps_ref[q, t : t + 1, :]
                re = re + tap * spec_ref[0, t + h : t + h + 64, :]
                im = im + tap * spec_ref[1, t + h : t + h + 64, :]
            rows = slice(h, h + 64)
            filt_ref[q, 0, rows] = re
            filt_ref[q, 1, rows] = im
            run = run_ref[0, rows] + jnp.where(low[:64] | (q > 0), re * re + im * im, 0.0)
            run_ref[0, rows] = run
            upto_ref[q, rows] = run

    run_ref[0] = jnp.zeros((BLK, 128), jnp.float32)
    second_stage(0, even_ref)

    @pl.loop(0, QT // 2)
    def _(h):
        second_stage(2 * h + 1, odd_ref)
        fan(2 * h, even_ref)
        second_stage(jnp.minimum(2 * h + 2, QT - 1), even_ref)
        fan(2 * h + 1, odd_ref)

    power = filt_ref[0, 0] * filt_ref[0, 0] + filt_ref[0, 1] * filt_ref[0, 1]
    run_ref[0] = run_ref[0] + jnp.where(low, 0.0, power)
    sums = run_ref[0]
    swapped = pltpu.roll(sums, 64, 1)
    total = sums + swapped
    run_ref[1] = total
    run_ref[2] = (
        total
        + jnp.where(k2 >= 1, pltpu.roll(total, 1, 1), 0.0)
        + jnp.where(k2 <= 62, pltpu.roll(total, 127, 1), 0.0)
    )
    run_ref[3] = jnp.where(low, power, sums)
    run_ref[4] = jnp.where(low, total, swapped + power)
    sign = 1 - 2 * core

    @pl.loop(0, QT)
    def _(step):
        to_x = (x + 4 + sign * (step % 4)) % 4
        to_z = (z + 4 + sign * ((step // 4 + 2 * step) % 4)) % 4
        q = to_x * 4 + to_z
        re, im = filt_ref[q, 0], filt_ref[q, 1]
        upto = jnp.where(q == 0, run_ref[3], upto_ref[q])
        rest = jnp.where(q == 0, run_ref[4], jnp.maximum(run_ref[1] - upto_ref[jnp.maximum(q - 1, 0)], 0.0))
        prefix = jnp.where(low, upto, rest)
        suffix = jnp.where(low, rest, upto)
        window = (
            run_ref[2]
            + jnp.where(k2 >= 2, pltpu.roll(suffix, 2, 1), 0.0)
            + jnp.where(k2 <= 61, pltpu.roll(prefix, 126, 1), 0.0)
        )
        scale = lax.rsqrt(window * rows_ref[2, pl.ds(q, 1), :] + EPSILON)
        cos = rows_ref[0, pl.ds(q, 1), :]
        sin = rows_ref[1, pl.ds(q, 1), :]
        white_re = ((re * cos + im * sin) * scale).astype(jnp.bfloat16).T
        white_im = ((im * cos - re * sin) * scale).astype(jnp.bfloat16).T
        tile = pl.ds(q * 8, 8)
        white_ref[tile, 0] = white_re.reshape(8, 16, 128)
        white_ref[tile, 1] = white_im.reshape(8, 16, 128)
        for dy in range(4):
            for dc in range(2):
                shard = (to_z * 4 + (y + 4 + sign * dy) % 4) * 2 + (core + dc) % 2

                def push():
                    copy_to(
                        white_ref.at[to_x * 32 + shard], bands_ref.at[me], band_send, band_recv, (to_x, shard)
                    ).start()

                if dy == 0 and dc == 0:
                    pl.when(step > 0)(push)
                else:
                    push()

    bands_ref[me] = white_ref[me]
    out_ref[...] = jnp.zeros_like(out_ref)
    somewhere = partner(1, False)
    others = pl.ds(0, NDEV - 1)
    copy_to(white_ref.at[others], bands_ref.at[others], band_send, band_recv, somewhere).wait()

    def products(owner, to_ref, slot):
        for p in range(4):
            a = pairs_ref[0, 4 * owner + p]
            b = pairs_ref[1, 4 * owner + p]
            left = bands_ref[a].astype(jnp.float32)
            right = pltpu.roll(bands_ref[b].astype(jnp.float32).reshape(32, 128), 64, 1).reshape(2, 16, 128)
            to_ref[slot, p, 0] = (left[0] * right[0] + left[1] * right[1]).astype(jnp.bfloat16)
            to_ref[slot, p, 1] = (left[1] * right[0] - left[0] * right[1]).astype(jnp.bfloat16)

    @pl.loop(1, NDEV)
    def _(i):
        group, shard = partner(i, False)
        products(group * 32 + shard, send_ref, i)
        copy_to(send_ref.at[i], recv_ref.at[i], cross_send, cross_recv.at[i // 8], (group, shard)).start()

    products(me, recv_ref, 0)

    def accumulate(first, count, g):
        some = pl.ds(first, count)
        copy_to(send_ref.at[some], recv_ref.at[some], cross_send, cross_recv.at[g], somewhere).wait_recv()
        slots = pl.ds(g * 8, 8)
        lags = lags_ref[slots].reshape(256, NLAG)
        for p in range(4):
            piece = recv_ref[slots, p].reshape(256, BLK)
            out_ref[p] += lax.dot_general(
                piece, lags, (((0,), (0,)), ((), ())), preferred_element_type=jnp.float32
            )

    accumulate(1, 7, 0)

    @pl.loop(1, 16)
    def _(g):
        accumulate(g * 8, 8, g)

    rest_of = pl.ds(1, NDEV - 1)
    copy_to(send_ref.at[rest_of], recv_ref.at[rest_of], cross_send, cross_recv.at[0], somewhere).wait_send()


def correlate(pairs, offsets, x, fan_taps, table):
    f32, bf16 = jnp.float32, jnp.bfloat16
    vmem = pl.BlockSpec(memory_space=pltpu.VMEM)
    smem = pl.BlockSpec(memory_space=pltpu.SMEM)
    return pl.pallas_call(
        kernel,
        out_shape=jax.ShapeDtypeStruct((4, BLK, NLAG), f32),
        in_specs=[smem, smem, vmem, vmem, pl.BlockSpec(memory_space=pl.ANY)],
        out_specs=vmem,
        scratch_shapes=[
            pltpu.VMEM((QT, 256, 256), bf16),
            pltpu.VMEM((2, HALF, NT), bf16),
            pltpu.VMEM((QT, WIDE, 256), bf16),
            pltpu.VMEM((2, WIDE, 128), f32),
            pltpu.VMEM((2, WIDE, 128), f32),
            pltpu.VMEM((NB, 128), f32),
            pltpu.VMEM((QT, 40, 128), f32),
            pltpu.VMEM((QT, 2, BLK, 128), f32),
            pltpu.VMEM((QT, BLK, 128), f32),
            pltpu.VMEM((5, BLK, 128), f32),
            pltpu.VMEM((3, QT, 128), f32),
            pltpu.VMEM((NDEV, 2, 16, BLK), bf16),
            pltpu.VMEM((NDEV, 2, 16, BLK), bf16),
            pltpu.VMEM((NDEV, 4, 2, 16, BLK), bf16),
            pltpu.VMEM((NDEV, 4, 2, 16, BLK), bf16),
            pltpu.VMEM((NDEV, 2, 16, NLAG), bf16),
            pltpu.VMEM((2, 32, NLAG), f32),
            pltpu.VMEM((2, 64, NLAG), f32),
            pltpu.SemaphoreType.DMA,
            pltpu.SemaphoreType.DMA((2,)),
            pltpu.SemaphoreType.DMA((2,)),
            pltpu.SemaphoreType.DMA,
            pltpu.SemaphoreType.DMA,
            pltpu.SemaphoreType.DMA,
            pltpu.SemaphoreType.DMA((16,)),
        ],
        compiler_params=pltpu.CompilerParams(collective_id=0, has_side_effects=True, vmem_limit_bytes=48 << 20),
        name="correlate",
    )(pairs, offsets, x, fan_taps, table)


def body(samples, fan_taps, pair_blocks, pair_valid, coil_offsets):
    table = jnp.asarray(second_stage_table())
    sums = correlate(pair_blocks.T, coil_offsets, samples.reshape(BLK, NT), fan_taps, table)
    weights = pair_valid.astype(jnp.float32) * (1.0 / math.sqrt(NB))
    return sums * weights[:, None, None]


def solution(mesh):
    return jax.shard_map(
        body,
        mesh=mesh,
        in_specs=(P(AXES, None, None), P(), P(), P(AXES), P()),
        out_specs=P(AXES, None, None),
        check_vma=False,
    )
```

time: 148 us -> 105 us (0.71)
  blocking collectives: 57.4 us -> 0 us
  Pallas kernels: 44.5 us -> 98.1 us
  waiting for transfers between devices: 21.4 us -> 0 us
  starting transfers between devices: 18.8 us -> 0 us
    all_to_all x1 -> x0, blocking collectives: 57.4 us -> none  [body(): lax.all_to_all(cross.reshape(NDEV, 4, 2, 16, BLK), AXES, split_axis=0, co...]
    pallas_call x3 -> x1, Pallas kernels: 44.5 us -> 98.1 us  [correlate(): pl.pallas_call(kernel, out_shape=jax.ShapeDtypeStruct((4, BLK, NLAG), f32...]
    all_to_all x1 -> x0, waiting for transfers between devices: 18.7 us -> none  [body(): bands = lax.all_to_all(white, AXES, split_axis=0, concat_axis=0, tiled=True)]
    all_to_all x1 -> x0, starting transfers between devices: 12.3 us -> none  [body(): bands = lax.all_to_all(white, AXES, split_axis=0, concat_axis=0, tiled=True)]
    ppermute x2 -> x0, starting transfers between devices: 6.5 us -> none  [the longest x1 4.58 us: body(): lax.ppermute(x[BLK - HALF:], AXES, [(i, i + 1) for i in range(NDEV - 1)])]
    unnamed x11 -> x10, local copies, waits for them, and re-layouts: 0.18 us -> 5.13 us
    ppermute x2 -> x0, waiting for transfers between devices: 2.62 us -> none  [the longest x1 2.61 us: body(): after = lax.ppermute(x[:HALF], AXES, [(i + 1, i) for i in range(NDEV - 1)])]
    reshape x3 -> x0, local copies, waits for them, and re-layouts: 1.92 us -> none  [the longest x2 1.75 us: body(): by_residue = fan_taps.reshape(TAPS, 64, 32).transpose(2, 0, 1)]
  transfers between devices with their start and end apart: 3 -> 0, of which waited for: 2 -> 0; matrix products, arithmetic and copies ran while one was open for 2% -> 0% of each run, Pallas kernels for 0% -> 0%
where the time goes in v3:
time: 105 us
  Pallas kernels  98.1 us (93%)
  local copies, waits for them, and re-layouts  5.13 us (5%)
  other arithmetic  1.82 us (2%)
    pallas_call x1, Pallas kernels, correlate(): pl.pallas_call(kernel, out_shape=jax.ShapeDtypeStruct((4, BLK, NLAG), f32...  98.1 us
    unnamed x10, local copies, waits for them, and re-layouts  5.13 us

profile of v3, /device:TPU:1, one launch (start us, length us, event | category | flops | bytes accessed | tf_op | source)
XLA Modules:
  0.0 105.1 jit_solution(10091359672411023472)
XLA Ops:
  0.0 0.7 convert_multiply_fusion
  0.7 0.0 copy-start
  0.7 1.6 %copy-done = bf16[16,256,256]{2,1,0:T(8,128)(2,1)S(1)} copy-done((bf16[16,256,256]{2,1,0:T(8,128)(2,1)S(1)}, bf16[16,256,256]{2,1,0:T(8,128)(2,1)}, u32[]{:S(2)}) %copy-start) | copy-done | bytes 2097176
  2.3 0.0 copy-start.1
  2.3 1.2 %copy-done.1 = bf16[128,1,4096]{2,0,1:T(8,128)(2,1)S(1)} copy-done((bf16[128,1,4096]{2,0,1:T(8,128)(2,1)S(1)}, bf16[128,1,4096]{2,0,1:T(8,128)(2,1)}, u32[]{:S(2)}) %copy-start.1) | copy-done | bytes 1048600
  3.5 0.0 copy-start.2
  3.5 1.0 copy-done.2
  4.4 0.0 copy-start.3
  4.5 0.7 copy-done.3
  5.1 0.0 copy-start.4
  5.1 0.7 copy-done.4
  5.8 98.1 %correlate.1 = f32[4,128,512]{2,1,0:T(8,128)S(1)} custom-call(s32[2,512]{1,0:T(2,128)S(1)} %bitcast.3, s32[128]{0:T(128)S(1)} %copy-done.4, bf16[128,4096]{1,0:T(8,128)(2,1)S(1)} %bitcast.2, f32[33,2048]{1,0:T(8,128)S(1)} %copy-done.2, bf16[16,256,256]{2,1,0:T(8,128)(2,1)S(1)} %copy-done), custom_call_target="tpu_custom_call" | custom-call | tf_op jit(solution)/shard_map/correlate/pallas_call | solution.py:366
  103.9 1.2 %broadcast_multiply_fusion = f32[4,128,512]{2,1,0:T(8,128)} fusion(f32[4,128,512]{2,1,0:T(8,128)S(1)} %correlate.1, f32[4]{0:T(128)S(1)} %convert_multiply_fusion), kind=kLoop, calls=%fused_computation | loop fusion | flops 262144 | bytes 2097168 | tf_op jit(solution)/shard_map/mul | solution.py:407
Async XLA Ops:
  0.7 1.6 %copy-start = (bf16[16,256,256]{2,1,0:T(8,128)(2,1)S(1)}, bf16[16,256,256]{2,1,0:T(8,128)(2,1)}, u32[]{:S(2)}) copy-start(bf16[16,256,256]{2,1,0:T(8,128)(2,1)} %constant.4.clone.table_hbm) | copy-start | bytes 6291460
  2.3 1.2 %copy-start.1 = (bf16[128,1,4096]{2,0,1:T(8,128)(2,1)S(1)}, bf16[128,1,4096]{2,0,1:T(8,128)(2,1)}, u32[]{:S(2)}) copy-start(bf16[128,1,4096]{2,0,1:T(8,128)(2,1)} %param.6) | copy-start | bytes 3145732
  3.5 1.0 copy-start.2
  4.4 0.7 copy-start.3
  5.1 0.7 copy-start.4

commit v4 on v3

--- a/solution.py
+++ b/solution.py
@@ -18,6 +18,7 @@
 EPSILON = 1e-05
 AXES = ("group", "shard")
 NDEV = 128
+PAIRS = 512
 MESH = pl.DeviceIdType.MESH
 TAPS = 2 * HALF + 1
 QT = 16
@@ -146,16 +147,20 @@
     coarse_ref[1] = jnp.sin(coarse[:32])
 
 
-def lag_rows(i, coarse_ref, fine_ref, lags_ref):
-    group, shard = partner(i, True)
-    band = group * 32 + shard
-    tile, part = band // 8, band % 8
-    residue = jnp.where(part < 4, tile, jnp.where(tile == 0, 16, 32 - tile))
-    cos_a, sin_a = coarse_ref[0, pl.ds(residue, 1), :], coarse_ref[1, pl.ds(residue, 1), :]
-    rows = pl.ds(pl.multiple_of(part % 4 * 16, 16), 16)
-    cos_b, sin_b = fine_ref[0, rows, :], fine_ref[1, rows, :]
-    lags_ref[i, 0] = (cos_a * cos_b - sin_a * sin_b).astype(jnp.bfloat16)
-    lags_ref[i, 1] = (-(sin_a * cos_b + cos_a * sin_b)).astype(jnp.bfloat16)
+def lag_rows(q, coarse_ref, fine_ref, lags_ref):
+    cos_b, sin_b = fine_ref[0], fine_ref[1]
+    for half, residue in ((0, q), (64, jnp.where(q == 0, 16, 32 - q))):
+        cos_a, sin_a = coarse_ref[0, pl.ds(residue, 1), :], coarse_ref[1, pl.ds(residue, 1), :]
+        lags_ref[q, half : half + 64] = (cos_a * cos_b - sin_a * sin_b).astype(jnp.bfloat16)
+        lags_ref[q, 128 + half : 192 + half] = (-(sin_a * cos_b + cos_a * sin_b)).astype(jnp.bfloat16)
+
+
+def pick_rows(pairs_ref, pick_ref):
+    block = lax.broadcasted_iota(jnp.int32, (128, 128), 0)
+    for side in range(2):
+        for at in range(0, PAIRS, 128):
+            chosen = block == pairs_ref[side : side + 1, at : at + 128]
+            pick_ref[side, at : at + 128, :] = jnp.where(chosen, 1.0, 0.0).T.astype(jnp.bfloat16)
 
 
 def bin_rows(offset, rows_ref):
@@ -176,17 +181,29 @@
     )
 
 
+def channel_of(device):
+    return device // 2 + 64 * (device % 2)
+
+
 def kernel(
-    pairs_ref, offsets_ref, x_ref, fan_ref, table_hbm, out_ref,
-    table_ref, halo_ref, y_ref, even_ref, odd_ref, turned_ref, taps_ref, filt_ref, upto_ref, run_ref, rows_ref,
-    white_ref, bands_ref, send_ref, recv_ref, lags_ref, coarse_ref, fine_ref,
-    table_sem, halo_send, halo_recv, band_send, band_recv, cross_send, cross_recv,
+    pairs_hbm, offsets_hbm, valid_hbm, x_hbm, fan_hbm, table_hbm, out_ref,
+    pairs_ref, offsets_ref, valid_ref, x_ref, fan_ref, table_ref,
+    halo_ref, y_ref, even_ref, odd_ref, turned_ref, taps_ref, filt_ref, upto_ref, run_ref, rows_ref,
+    rows32_ref, white_ref, blocks_ref, own_ref, other_ref, pick_ref, cross_ref, sums_ref,
+    parts_ref, recv_ref, lags_ref, coarse_ref, fine_ref,
+    fetch_sem, halo_send, halo_recv, block_send, block_recv, swap_send, swap_recv, part_send, part_recv,
 ):
     x, z, y, core = place()
     me = lax.axis_index("group") * 32 + lax.axis_index("shard")
     barrier = pltpu.get_barrier_semaphore()
-    fetch = pltpu.make_async_copy(table_hbm, table_ref, table_sem)
-    fetch.start()
+    moves = (
+        (x_hbm, x_ref), (offsets_hbm, offsets_ref), (fan_hbm, fan_ref),
+        (pairs_hbm, pairs_ref), (valid_hbm, valid_ref), (table_hbm, table_ref),
+    )
+    fetches = [pltpu.make_async_copy(src, dst, fetch_sem.at[n]) for n, (src, dst) in enumerate(moves)]
+    for fetch in fetches:
+        fetch.start()
+    fetches[0].wait()
 
     @pl.loop(0, 8)
     def _(chunk):
@@ -209,13 +226,16 @@
     to_after.start()
     to_before.start()
 
+    for fetch in fetches[1:5]:
+        fetch.wait()
     sort_taps(fan_ref, turned_ref, taps_ref)
     bin_rows(offsets_ref[me], rows_ref)
     lag_tables(coarse_ref, fine_ref)
-
-    @pl.loop(0, NDEV)
-    def _(i):
-        lag_rows(i, coarse_ref, fine_ref, lags_ref)
+    pick_rows(pairs_ref, pick_ref)
+
+    @pl.loop(0, QT)
+    def _(q):
+        lag_rows(q, coarse_ref, fine_ref, lags_ref)
 
     to_after.wait()
     to_before.wait()
@@ -228,7 +248,7 @@
             [halo_ref[side, :, a * 128 : (a + 1) * 128].astype(jnp.float32) * edge for a in range(32)], y_ref, to
         )
 
-    fetch.wait()
+    fetches[5].wait()
     lanes = lax.broadcasted_iota(jnp.int32, (BLK, 128), 1)
     low = lanes < 64
     k2 = lanes & 63
@@ -276,13 +296,9 @@
     )
     run_ref[3] = jnp.where(low, power, sums)
     run_ref[4] = jnp.where(low, total, swapped + power)
-    sign = 1 - 2 * core
 
     @pl.loop(0, QT)
-    def _(step):
-        to_x = (x + 4 + sign * (step % 4)) % 4
-        to_z = (z + 4 + sign * ((step // 4 + 2 * step) % 4)) % 4
-        q = to_x * 4 + to_z
+    def _(q):
         re, im = filt_ref[q, 0], filt_ref[q, 1]
         upto = jnp.where(q == 0, run_ref[3], upto_ref[q])
         rest = jnp.where(q == 0, run_ref[4], jnp.maximum(run_ref[1] - upto_ref[jnp.maximum(q - 1, 0)], 0.0))
@@ -296,79 +312,117 @@
         scale = lax.rsqrt(window * rows_ref[2, pl.ds(q, 1), :] + EPSILON)
         cos = rows_ref[0, pl.ds(q, 1), :]
         sin = rows_ref[1, pl.ds(q, 1), :]
-        white_re = ((re * cos + im * sin) * scale).astype(jnp.bfloat16).T
-        white_im = ((im * cos - re * sin) * scale).astype(jnp.bfloat16).T
-        tile = pl.ds(q * 8, 8)
-        white_ref[tile, 0] = white_re.reshape(8, 16, 128)
-        white_ref[tile, 1] = white_im.reshape(8, 16, 128)
-        for dy in range(4):
-            for dc in range(2):
-                shard = (to_z * 4 + (y + 4 + sign * dy) % 4) * 2 + (core + dc) % 2
-
-                def push():
-                    copy_to(
-                        white_ref.at[to_x * 32 + shard], bands_ref.at[me], band_send, band_recv, (to_x, shard)
-                    ).start()
-
-                if dy == 0 and dc == 0:
-                    pl.when(step > 0)(push)
-                else:
-                    push()
-
-    bands_ref[me] = white_ref[me]
-    out_ref[...] = jnp.zeros_like(out_ref)
-    somewhere = partner(1, False)
-    others = pl.ds(0, NDEV - 1)
-    copy_to(white_ref.at[others], bands_ref.at[others], band_send, band_recv, somewhere).wait()
-
-    def products(owner, to_ref, slot):
-        for p in range(4):
-            a = pairs_ref[0, 4 * owner + p]
-            b = pairs_ref[1, 4 * owner + p]
-            left = bands_ref[a].astype(jnp.float32)
-            right = pltpu.roll(bands_ref[b].astype(jnp.float32).reshape(32, 128), 64, 1).reshape(2, 16, 128)
-            to_ref[slot, p, 0] = (left[0] * right[0] + left[1] * right[1]).astype(jnp.bfloat16)
-            to_ref[slot, p, 1] = (left[1] * right[0] - left[0] * right[1]).astype(jnp.bfloat16)
+        rows32_ref[pl.ds(q, BLK, stride=32), :] = (re * cos + im * sin) * scale
+        rows32_ref[pl.ds(16 + q, BLK, stride=32), :] = (im * cos - re * sin) * scale
+
+    def packed(channel):
+        return rows32_ref[pl.ds(pl.multiple_of(channel * 32, 32), 32), :].astype(jnp.bfloat16)
 
     @pl.loop(1, NDEV)
     def _(i):
         group, shard = partner(i, False)
-        products(group * 32 + shard, send_ref, i)
-        copy_to(send_ref.at[i], recv_ref.at[i], cross_send, cross_recv.at[i // 8], (group, shard)).start()
-
-    products(me, recv_ref, 0)
-
-    def accumulate(first, count, g):
-        some = pl.ds(first, count)
-        copy_to(send_ref.at[some], recv_ref.at[some], cross_send, cross_recv.at[g], somewhere).wait_recv()
-        slots = pl.ds(g * 8, 8)
-        lags = lags_ref[slots].reshape(256, NLAG)
-        for p in range(4):
-            piece = recv_ref[slots, p].reshape(256, BLK)
-            out_ref[p] += lax.dot_general(
-                piece, lags, (((0,), (0,)), ((), ())), preferred_element_type=jnp.float32
-            )
-
-    accumulate(1, 7, 0)
-
-    @pl.loop(1, 16)
-    def _(g):
-        accumulate(g * 8, 8, g)
-
-    rest_of = pl.ds(1, NDEV - 1)
-    copy_to(send_ref.at[rest_of], recv_ref.at[rest_of], cross_send, cross_recv.at[0], somewhere).wait_send()
-
-
-def correlate(pairs, offsets, x, fan_taps, table):
-    f32, bf16 = jnp.float32, jnp.bfloat16
-    vmem = pl.BlockSpec(memory_space=pltpu.VMEM)
-    smem = pl.BlockSpec(memory_space=pltpu.SMEM)
+        channel = channel_of(group * 32 + shard)
+        white_ref[channel] = packed(channel)
+        copy_to(white_ref.at[channel], blocks_ref.at[me], block_send, block_recv, (group, shard)).start()
+
+    mine = channel_of(me)
+    blocks_ref[me] = packed(mine)
+    somewhere = partner(1, False)
+    others = pl.ds(0, NDEV - 1)
+    copy_to(white_ref.at[others], blocks_ref.at[others], block_send, block_recv, somewhere).wait()
+
+    sibling = (lax.axis_index("group"), lax.axis_index("shard") + 1 - 2 * core)
+
+    @pl.loop(0, NDEV // 8)
+    def _(d):
+        eight = pl.ds(pl.multiple_of(d * 8, 8), 8)
+        to = pl.ds(pl.multiple_of(d * 256, 256), 256)
+        rows32_ref[to, :] = blocks_ref[eight].reshape(256, 128).astype(jnp.float32)
+
+    def swap(part):
+        some = pl.ds(part * 4, 4)
+        return copy_to(own_ref.at[some], other_ref.at[some], swap_send.at[part], swap_recv.at[part], sibling)
+
+    @pl.loop(0, 4)
+    def _(part):
+        for n in range(4):
+            q = part * 4 + n
+            own_ref[q, :, 0:128] = rows32_ref[pl.ds(q, BLK, stride=32), :].astype(jnp.bfloat16)
+            own_ref[q, :, 128:256] = rows32_ref[pl.ds(16 + q, BLK, stride=32), :].astype(jnp.bfloat16)
+        swap(part).start()
+
+    def add_part(part, half):
+        rows = pl.ds(pl.multiple_of(half * 256, 256), 256)
+        for n in range(4):
+            q = part * 4 + n
+            left = jnp.dot(pick_ref[0, rows, :], own_ref[q], preferred_element_type=jnp.float32)
+            right = jnp.dot(pick_ref[1, rows, :], other_ref[q], preferred_element_type=jnp.float32)
+            l_re, l_im, r_re, r_im = left[:, :128], left[:, 128:], right[:, :128], right[:, 128:]
+            cross_ref[:, n * 256 : n * 256 + 128] = (l_re * r_re + l_im * r_im).astype(jnp.bfloat16)
+            cross_ref[:, n * 256 + 128 : n * 256 + 256] = (l_im * r_re - l_re * r_im).astype(jnp.bfloat16)
+        lags = lags_ref[pl.ds(part * 4, 4)].reshape(1024, NLAG)
+        return jnp.dot(cross_ref[...], lags, preferred_element_type=jnp.float32)
+
+    @pl.loop(0, 3)
+    def _(part):
+        swap(part).wait()
+        for half in range(2):
+            rows = slice(half * 256, half * 256 + 256)
+            added = add_part(part, half)
+            sums_ref[rows, :] = jnp.where(part == 0, added, sums_ref[rows, :] + added)
+
+    swap(3).wait()
+
+    @pl.loop(0, 2)
+    def _(turn):
+        half = (turn + y) % 2
+        rows = pl.ds(pl.multiple_of(half * 256, 256), 256)
+        done = sums_ref[rows, :] + add_part(3, half)
+        for n in range(4):
+            rows32_ref[pl.ds(half * 1024 + n, 256, stride=4), :] = done[:, n * 128 : n * 128 + 128]
+
+        @pl.loop(0, 64)
+        def _(i):
+            to_x = 2 * half + (x + i) % 2
+            to_y = (y + i // 2 + i) % 4
+            to_z = (z + i // 8 + i) % 4
+            shard = (to_z * 4 + to_y) * 2 + (core + i // 32) % 2
+            owner = to_x * 32 + shard
+            part = rows32_ref[pl.ds(pl.multiple_of(owner * 16, 16), 16), :].astype(jnp.bfloat16)
+            parts_ref[owner] = part
+
+            @pl.when(owner != me)
+            def _():
+                copy_to(parts_ref.at[owner], recv_ref.at[mine], part_send, part_recv, (to_x, shard)).start()
+
+    recv_ref[mine] = parts_ref[me]
+    copy_to(parts_ref.at[others], recv_ref.at[others], part_send, part_recv, somewhere).wait()
+
+    @pl.loop(0, NDEV // 16)
+    def _(d):
+        some = pl.ds(pl.multiple_of(d * 16, 16), 16)
+        to = pl.ds(pl.multiple_of(d * 256, 256), 256)
+        rows32_ref[to, :] = recv_ref[some].reshape(256, 128).astype(jnp.float32)
+
+    for p in range(4):
+        weight = valid_ref[p].astype(jnp.float32) * (1.0 / math.sqrt(NB))
+        for n in range(4):
+            out_ref[p, :, n * 128 : n * 128 + 128] = rows32_ref[pl.ds(p * 4 + n, BLK, stride=16), :] * weight
+
+
+def correlate(*operands):
+    f32, bf16, i32 = jnp.float32, jnp.bfloat16, jnp.int32
     return pl.pallas_call(
         kernel,
         out_shape=jax.ShapeDtypeStruct((4, BLK, NLAG), f32),
-        in_specs=[smem, smem, vmem, vmem, pl.BlockSpec(memory_space=pl.ANY)],
-        out_specs=vmem,
+        in_specs=[pl.BlockSpec(memory_space=pltpu.HBM)] * 6,
+        out_specs=pl.BlockSpec(memory_space=pltpu.VMEM),
         scratch_shapes=[
+            pltpu.VMEM((2, PAIRS), i32),
+            pltpu.SMEM((NDEV,), i32),
+            pltpu.SMEM((4,), i32),
+            pltpu.VMEM((BLK, NT), bf16),
+            pltpu.VMEM((TAPS, NB), f32),
             pltpu.VMEM((QT, 256, 256), bf16),
             pltpu.VMEM((2, HALF, NT), bf16),
             pltpu.VMEM((QT, WIDE, 256), bf16),
@@ -380,31 +434,37 @@
             pltpu.VMEM((QT, BLK, 128), f32),
             pltpu.VMEM((5, BLK, 128), f32),
             pltpu.VMEM((3, QT, 128), f32),
-            pltpu.VMEM((NDEV, 2, 16, BLK), bf16),
-            pltpu.VMEM((NDEV, 2, 16, BLK), bf16),
-            pltpu.VMEM((NDEV, 4, 2, 16, BLK), bf16),
-            pltpu.VMEM((NDEV, 4, 2, 16, BLK), bf16),
-            pltpu.VMEM((NDEV, 2, 16, NLAG), bf16),
+            pltpu.VMEM((32 * BLK, 128), f32),
+            pltpu.VMEM((NDEV, 32, 128), bf16),
+            pltpu.VMEM((NDEV, 32, 128), bf16),
+            pltpu.VMEM((QT, NDEV, 256), bf16),
+            pltpu.VMEM((QT, NDEV, 256), bf16),
+            pltpu.VMEM((2, PAIRS, NDEV), bf16),
+            pltpu.VMEM((256, 1024), bf16),
+            pltpu.VMEM((PAIRS, NLAG), f32),
+            pltpu.VMEM((NDEV, 16, 128), bf16),
+            pltpu.VMEM((NDEV, 16, 128), bf16),
+            pltpu.VMEM((QT, 256, NLAG), bf16),
             pltpu.VMEM((2, 32, NLAG), f32),
             pltpu.VMEM((2, 64, NLAG), f32),
-            pltpu.SemaphoreType.DMA,
+            pltpu.SemaphoreType.DMA((6,)),
             pltpu.SemaphoreType.DMA((2,)),
             pltpu.SemaphoreType.DMA((2,)),
             pltpu.SemaphoreType.DMA,
             pltpu.SemaphoreType.DMA,
+            pltpu.SemaphoreType.DMA((4,)),
+            pltpu.SemaphoreType.DMA((4,)),
             pltpu.SemaphoreType.DMA,
-            pltpu.SemaphoreType.DMA((16,)),
+            pltpu.SemaphoreType.DMA,
         ],
         compiler_params=pltpu.CompilerParams(collective_id=0, has_side_effects=True, vmem_limit_bytes=48 << 20),
         name="correlate",
-    )(pairs, offsets, x, fan_taps, table)
+    )(*operands)
 
 
 def body(samples, fan_taps, pair_blocks, pair_valid, coil_offsets):
     table = jnp.asarray(second_stage_table())
-    sums = correlate(pair_blocks.T, coil_offsets, samples.reshape(BLK, NT), fan_taps, table)
-    weights = pair_valid.astype(jnp.float32) * (1.0 / math.sqrt(NB))
-    return sums * weights[:, None, None]
+    return correlate(pair_blocks.T, coil_offsets, pair_valid, samples.reshape(BLK, NT), fan_taps, table)
 
 
 def solution(mesh):

time: 105 us -> 71.1 us (0.68)
  Pallas kernels: 98.1 us -> 64 us
  other arithmetic: 1.82 us -> 0 us
  local copies, waits for them, and re-layouts: 5.13 us -> 6.76 us
    pallas_call x1, Pallas kernels: 98.1 us -> 64 us  [correlate(): pl.pallas_call(kernel, out_shape=jax.ShapeDtypeStruct((4, BLK, NLAG), f32...]
    mul x2 -> x0, other arithmetic: 1.82 us -> none  [the longest x1 1.16 us: body(): return sums * weights[:, None, None]]
    unnamed x10 -> x13, local copies, waits for them, and re-layouts: 5.13 us -> 6.76 us
where the time goes in v4:
time: 71.1 us; the launch traced here: 70.8 us
  Pallas kernels  64 us (90%)
  local copies, waits for them, and re-layouts  6.76 us (10%)
    pallas_call x1, Pallas kernels, correlate(): pl.pallas_call(kernel, out_shape=jax.ShapeDtypeStruct((4, BLK, NLAG), f32...  64 us
    unnamed x13, local copies, waits for them, and re-layouts  6.76 us

profile of v4, /device:TPU:1, one launch (start us, length us, event | category | flops | bytes accessed | tf_op | source)
XLA Modules:
  0.0 70.8 jit_solution(8425635312969773173)
XLA Ops:
  0.0 0.0 copy-start
  0.0 1.6 %copy-done = bf16[16,256,256]{2,1,0:T(8,128)(2,1)S(1)} copy-done((bf16[16,256,256]{2,1,0:T(8,128)(2,1)S(1)}, bf16[16,256,256]{2,1,0:T(8,128)(2,1)}, u32[]{:S(2)}) %copy-start) | copy-done | bytes 2097176
  1.6 0.0 copy-start.1
  1.6 1.2 %copy-done.1 = bf16[128,1,4096]{2,0,1:T(8,128)(2,1)S(1)} copy-done((bf16[128,1,4096]{2,0,1:T(8,128)(2,1)S(1)}, bf16[128,1,4096]{2,0,1:T(8,128)(2,1)}, u32[]{:S(2)}) %copy-start.1) | copy-done | bytes 1048600
  2.8 0.0 copy-start.2
  2.8 1.0 %copy-done.2 = f32[33,2048]{1,0:T(8,128)S(1)} copy-done((f32[33,2048]{1,0:T(8,128)S(1)}, f32[33,2048]{1,0:T(8,128)}, u32[]{:S(2)}) %copy-start.2) | copy-done | bytes 270360
  3.8 0.0 copy-start.3
  3.8 0.7 copy-done.3
  4.5 0.0 copy-start.4
  4.5 0.7 copy-done.4
  5.1 0.0 copy-start.5
  5.1 0.7 copy-done.5
  5.8 64.0 %correlate.1 = f32[4,128,512]{2,1,0:T(8,128)S(1)} custom-call(s32[2,512]{1,0:T(2,128)S(1)} %bitcast.3, s32[128]{0:T(128)S(1)} %copy-done.4, s32[4]{0:T(128)S(1)} %copy-done.5, bf16[128,4096]{1,0:T(8,128)(2,1)S(1)} %bitcast.2, f32[33,2048]{1,0:T(8,128)S(1)} %copy-done.2, bf16[16,256,256]{2,1,0:T(8,128)(2,1)S(1)} %copy-done), custom_call_target="tpu_custom_call" | custom-call | tf_op jit(solution)/shard_map/correlate/pallas_call | solution.py:415
  69.8 1.0 %copy.8 = f32[4,128,512]{2,1,0:T(8,128)} copy(f32[4,128,512]{2,1,0:T(8,128)S(1)} %correlate.1) | data formatting | bytes 2097152
Async XLA Ops:
  0.0 1.6 %copy-start = (bf16[16,256,256]{2,1,0:T(8,128)(2,1)S(1)}, bf16[16,256,256]{2,1,0:T(8,128)(2,1)}, u32[]{:S(2)}) copy-start(bf16[16,256,256]{2,1,0:T(8,128)(2,1)} %constant.2.clone.table_hbm) | copy-start | bytes 6291460
  1.6 1.2 %copy-start.1 = (bf16[128,1,4096]{2,0,1:T(8,128)(2,1)S(1)}, bf16[128,1,4096]{2,0,1:T(8,128)(2,1)}, u32[]{:S(2)}) copy-start(bf16[128,1,4096]{2,0,1:T(8,128)(2,1)} %param.6) | copy-start | bytes 3145732
  2.8 1.0 %copy-start.2 = (f32[33,2048]{1,0:T(8,128)S(1)}, f32[33,2048]{1,0:T(8,128)}, u32[]{:S(2)}) copy-start(f32[33,2048]{1,0:T(8,128)} %fan_hbm.1) | copy-start | bytes 811012
  3.8 0.7 copy-start.3
  4.5 0.7 copy-start.4
  5.1 0.7 copy-start.5

commit v5 on v4

--- a/solution.py
+++ b/solution.py
@@ -19,6 +19,7 @@
 AXES = ("group", "shard")
 NDEV = 128
 PAIRS = 512
+CHUNK = 32
 MESH = pl.DeviceIdType.MESH
 TAPS = 2 * HALF + 1
 QT = 16
@@ -77,21 +78,13 @@
     return out
 
 
-def offsets_of(i):
-    return i % 4, (i // 4 + 2 * i) % 4, (i // 16 + 3 * i) % 4, i // 64
-
-
 def place():
     shard = lax.axis_index("shard")
     return lax.axis_index("group"), shard // 8, (shard // 2) % 4, shard % 2
 
 
-def partner(i, back):
-    x, z, y, core = place()
-    dx, dz, dy, dc = offsets_of(i)
-    other = (core + dc) % 2
-    sign = 2 * other - 1 if back else 1 - 2 * core
-    return (x + 4 + sign * dx) % 4, ((z + 4 + sign * dz) % 4 * 4 + (y + 4 + sign * dy) % 4) * 2 + other
+def wrap(value, size):
+    return lax.rem(value, size)
 
 
 def signal_some(barrier, i):
@@ -181,14 +174,14 @@
     )
 
 
-def channel_of(device):
-    return device // 2 + 64 * (device % 2)
+def channel_of(x, z, y, core):
+    return wrap(x + z + y, 2) * 32 + (x * 16 + z * 4 + y) // 2 + 64 * core
 
 
 def kernel(
     pairs_hbm, offsets_hbm, valid_hbm, x_hbm, fan_hbm, table_hbm, out_ref,
     pairs_ref, offsets_ref, valid_ref, x_ref, fan_ref, table_ref,
-    halo_ref, y_ref, even_ref, odd_ref, turned_ref, taps_ref, filt_ref, upto_ref, run_ref, rows_ref,
+    halo_ref, y_ref, spec_ref, turned_ref, taps_ref, filt_ref, upto_ref, run_ref, rows_ref,
     rows32_ref, white_ref, blocks_ref, own_ref, other_ref, pick_ref, cross_ref, sums_ref,
     parts_ref, recv_ref, lags_ref, coarse_ref, fine_ref,
     fetch_sem, halo_send, halo_recv, block_send, block_recv, swap_send, swap_recv, part_send, part_recv,
@@ -213,23 +206,133 @@
         to = pl.ds(pl.multiple_of(chunk * 16 + 16, 16), 16)
         first_stage([x_ref[at, a * 128 : (a + 1) * 128].astype(jnp.float32) for a in range(32)], y_ref, to)
 
+    for fetch in fetches[1:]:
+        fetch.wait()
+    sort_taps(fan_ref, turned_ref, taps_ref)
+    bin_rows(offsets_ref[me], rows_ref)
+
+    def second_stage(rows):
+        @pl.loop(0, QT)
+        def _(q):
+            both = jnp.dot(y_ref[q, rows], table_ref[q], preferred_element_type=jnp.float32)
+            spec_ref[q, 0, rows] = both[:, :128]
+            spec_ref[q, 1, rows] = both[:, 128:]
+
+    second_stage(pl.ds(HALF, BLK))
+
     pl.semaphore_wait(barrier, NDEV - 1)
-    after, before = (me + 1) % NDEV, (me + NDEV - 1) % NDEV
+    after, before = wrap(me + 1, NDEV), wrap(me + NDEV - 1, NDEV)
     to_after = copy_to(
         x_ref.at[pl.ds(BLK - HALF, HALF)], halo_ref.at[0], halo_send.at[0], halo_recv.at[0],
-        (after // 32, after % 32),
+        (after // 32, wrap(after, 32)),
     )
     to_before = copy_to(
         x_ref.at[pl.ds(0, HALF)], halo_ref.at[1], halo_send.at[1], halo_recv.at[1],
-        (before // 32, before % 32),
+        (before // 32, wrap(before, 32)),
     )
     to_after.start()
     to_before.start()
 
-    for fetch in fetches[1:5]:
-        fetch.wait()
-    sort_taps(fan_ref, turned_ref, taps_ref)
-    bin_rows(offsets_ref[me], rows_ref)
+    def take_halo():
+        to_after.wait()
+        to_before.wait()
+
+        @pl.loop(0, 2)
+        def _(side):
+            edge = jnp.where(side == 0, me > 0, me < NDEV - 1).astype(jnp.float32)
+            to = pl.ds(pl.multiple_of(side * (BLK + HALF), 16), 16)
+            first_stage(
+                [halo_ref[side, :, a * 128 : (a + 1) * 128].astype(jnp.float32) * edge for a in range(32)],
+                y_ref,
+                to,
+            )
+
+        second_stage(pl.ds(0, HALF))
+        second_stage(pl.ds(BLK + HALF, HALF))
+
+    lanes = lax.broadcasted_iota(jnp.int32, (CHUNK, 128), 1)
+    low = lanes < 64
+    k2 = lanes & 63
+    sign = 1 - 2 * core
+    mine = channel_of(x, z, y, core)
+    somewhere = (x, lax.axis_index("shard") + 1 - 2 * core)
+    others = pl.ds(0, NDEV - 1)
+
+    @pl.loop(0, 4)
+    def _(turn):
+        pl.when(turn == 2)(take_halo)
+        ahead = jnp.where(turn < 2, 1 + turn, 3 * turn - 6)
+        chunk = jnp.where(core == 0, ahead, 3 - ahead)
+        first = pl.multiple_of(chunk * CHUNK, CHUNK)
+
+        def fan(q, run):
+            re = jnp.zeros((CHUNK, 128), jnp.float32)
+            im = re
+            for t in range(TAPS):
+                tap = taps_ref[q, t : t + 1, :]
+                re = re + tap * spec_ref[q, 0, pl.ds(first + t, CHUNK), :]
+                im = im + tap * spec_ref[q, 1, pl.ds(first + t, CHUNK), :]
+            filt_ref[q, 0] = re
+            filt_ref[q, 1] = im
+            run = run + jnp.where(low | (q > 0), re * re + im * im, 0.0)
+            upto_ref[q] = run
+            return run
+
+        run = lax.fori_loop(0, QT, fan, jnp.zeros((CHUNK, 128), jnp.float32))
+
+        power = filt_ref[0, 0] * filt_ref[0, 0] + filt_ref[0, 1] * filt_ref[0, 1]
+        sums = run + jnp.where(low, 0.0, power)
+        swapped = pltpu.roll(sums, 64, 1)
+        total = sums + swapped
+        run_ref[1] = total
+        run_ref[2] = (
+            total
+            + jnp.where(k2 >= 1, pltpu.roll(total, 1, 1), 0.0)
+            + jnp.where(k2 <= 62, pltpu.roll(total, 127, 1), 0.0)
+        )
+        run_ref[3] = jnp.where(low, power, sums)
+        run_ref[4] = jnp.where(low, total, swapped + power)
+
+        @pl.loop(0, QT, unroll=2)
+        def _(q):
+            re, im = filt_ref[q, 0], filt_ref[q, 1]
+            upto = jnp.where(q == 0, run_ref[3], upto_ref[q])
+            rest = jnp.where(q == 0, run_ref[4], jnp.maximum(run_ref[1] - upto_ref[jnp.maximum(q - 1, 0)], 0.0))
+            prefix = jnp.where(low, upto, rest)
+            suffix = jnp.where(low, rest, upto)
+            window = (
+                run_ref[2]
+                + jnp.where(k2 >= 2, pltpu.roll(suffix, 2, 1), 0.0)
+                + jnp.where(k2 <= 61, pltpu.roll(prefix, 126, 1), 0.0)
+            )
+            scale = lax.rsqrt(window * rows_ref[2, pl.ds(q, 1), :] + EPSILON)
+            cos = rows_ref[0, pl.ds(q, 1), :]
+            sin = rows_ref[1, pl.ds(q, 1), :]
+            rows32_ref[pl.ds(q, CHUNK, stride=32), :] = (re * cos + im * sin) * scale
+            rows32_ref[pl.ds(16 + q, CHUNK, stride=32), :] = (im * cos - re * sin) * scale
+
+        to_core, parity = chunk // 2, wrap(chunk, 2)
+
+        @pl.loop(0, 8)
+        def _(i):
+            to_y2 = wrap(y // 2 + i // 4, 2)
+            for dx in range(4):
+                to_x = wrap(x + 4 + sign * dx, 4)
+                to_z = wrap(z + 4 + sign * wrap(i + dx, 4), 4)
+                to_y = 2 * to_y2 + wrap(parity + to_x + to_z, 2)
+                shard = (to_z * 4 + to_y) * 2 + to_core
+                channel = channel_of(to_x, to_z, to_y, to_core)
+                at = pl.multiple_of((channel - first) * 32, 32)
+                white_ref[channel] = rows32_ref[pl.ds(at, 32), :].astype(jnp.bfloat16)
+
+                @pl.when(channel != mine)
+                def _():
+                    copy_to(
+                        white_ref.at[channel], blocks_ref.at[me], block_send, block_recv, (to_x, shard)
+                    ).start()
+
+    blocks_ref[me] = white_ref[mine]
+
     lag_tables(coarse_ref, fine_ref)
     pick_rows(pairs_ref, pick_ref)
 
@@ -237,101 +340,7 @@
     def _(q):
         lag_rows(q, coarse_ref, fine_ref, lags_ref)
 
-    to_after.wait()
-    to_before.wait()
-
-    @pl.loop(0, 2)
-    def _(side):
-        edge = jnp.where(side == 0, me > 0, me < NDEV - 1).astype(jnp.float32)
-        to = pl.ds(pl.multiple_of(side * (BLK + HALF), 16), 16)
-        first_stage(
-            [halo_ref[side, :, a * 128 : (a + 1) * 128].astype(jnp.float32) * edge for a in range(32)], y_ref, to
-        )
-
-    fetches[5].wait()
-    lanes = lax.broadcasted_iota(jnp.int32, (BLK, 128), 1)
-    low = lanes < 64
-    k2 = lanes & 63
-
-    def second_stage(q, to_ref):
-        both = jnp.dot(y_ref[q], table_ref[q], preferred_element_type=jnp.float32)
-        to_ref[0] = both[:, :128]
-        to_ref[1] = both[:, 128:]
-
-    def fan(q, spec_ref):
-        for h in (0, 64):
-            re = jnp.zeros((64, 128), jnp.float32)
-            im = re
-            for t in range(TAPS):
-                tap = taps_ref[q, t : t + 1, :]
-                re = re + tap * spec_ref[0, t + h : t + h + 64, :]
-                im = im + tap * spec_ref[1, t + h : t + h + 64, :]
-            rows = slice(h, h + 64)
-            filt_ref[q, 0, rows] = re
-            filt_ref[q, 1, rows] = im
-            run = run_ref[0, rows] + jnp.where(low[:64] | (q > 0), re * re + im * im, 0.0)
-            run_ref[0, rows] = run
-            upto_ref[q, rows] = run
-
-    run_ref[0] = jnp.zeros((BLK, 128), jnp.float32)
-    second_stage(0, even_ref)
-
-    @pl.loop(0, QT // 2)
-    def _(h):
-        second_stage(2 * h + 1, odd_ref)
-        fan(2 * h, even_ref)
-        second_stage(jnp.minimum(2 * h + 2, QT - 1), even_ref)
-        fan(2 * h + 1, odd_ref)
-
-    power = filt_ref[0, 0] * filt_ref[0, 0] + filt_ref[0, 1] * filt_ref[0, 1]
-    run_ref[0] = run_ref[0] + jnp.where(low, 0.0, power)
-    sums = run_ref[0]
-    swapped = pltpu.roll(sums, 64, 1)
-    total = sums + swapped
-    run_ref[1] = total
-    run_ref[2] = (
-        total
-        + jnp.where(k2 >= 1, pltpu.roll(total, 1, 1), 0.0)
-        + jnp.where(k2 <= 62, pltpu.roll(total, 127, 1), 0.0)
-    )
-    run_ref[3] = jnp.where(low, power, sums)
-    run_ref[4] = jnp.where(low, total, swapped + power)
-
-    @pl.loop(0, QT)
-    def _(q):
-        re, im = filt_ref[q, 0], filt_ref[q, 1]
-        upto = jnp.where(q == 0, run_ref[3], upto_ref[q])
-        rest = jnp.where(q == 0, run_ref[4], jnp.maximum(run_ref[1] - upto_ref[jnp.maximum(q - 1, 0)], 0.0))
-        prefix = jnp.where(low, upto, rest)
-        suffix = jnp.where(low, rest, upto)
-        window = (
-            run_ref[2]
-            + jnp.where(k2 >= 2, pltpu.roll(suffix, 2, 1), 0.0)
-            + jnp.where(k2 <= 61, pltpu.roll(prefix, 126, 1), 0.0)
-        )
-        scale = lax.rsqrt(window * rows_ref[2, pl.ds(q, 1), :] + EPSILON)
-        cos = rows_ref[0, pl.ds(q, 1), :]
-        sin = rows_ref[1, pl.ds(q, 1), :]
-        rows32_ref[pl.ds(q, BLK, stride=32), :] = (re * cos + im * sin) * scale
-        rows32_ref[pl.ds(16 + q, BLK, stride=32), :] = (im * cos - re * sin) * scale
-
-    def packed(channel):
-        return rows32_ref[pl.ds(pl.multiple_of(channel * 32, 32), 32), :].astype(jnp.bfloat16)
-
-    @pl.loop(1, NDEV)
-    def _(i):
-        group, shard = partner(i, False)
-        channel = channel_of(group * 32 + shard)
-        white_ref[channel] = packed(channel)
-        copy_to(white_ref.at[channel], blocks_ref.at[me], block_send, block_recv, (group, shard)).start()
-
-    mine = channel_of(me)
-    blocks_ref[me] = packed(mine)
-    somewhere = partner(1, False)
-    others = pl.ds(0, NDEV - 1)
     copy_to(white_ref.at[others], blocks_ref.at[others], block_send, block_recv, somewhere).wait()
-
-    sibling = (lax.axis_index("group"), lax.axis_index("shard") + 1 - 2 * core)
 
     @pl.loop(0, NDEV // 8)
     def _(d):
@@ -341,7 +350,7 @@
 
     def swap(part):
         some = pl.ds(part * 4, 4)
-        return copy_to(own_ref.at[some], other_ref.at[some], swap_send.at[part], swap_recv.at[part], sibling)
+        return copy_to(own_ref.at[some], other_ref.at[some], swap_send.at[part], swap_recv.at[part], somewhere)
 
     @pl.loop(0, 4)
     def _(part):
@@ -363,37 +372,33 @@
         lags = lags_ref[pl.ds(part * 4, 4)].reshape(1024, NLAG)
         return jnp.dot(cross_ref[...], lags, preferred_element_type=jnp.float32)
 
-    @pl.loop(0, 3)
-    def _(part):
-        swap(part).wait()
-        for half in range(2):
-            rows = slice(half * 256, half * 256 + 256)
-            added = add_part(part, half)
-            sums_ref[rows, :] = jnp.where(part == 0, added, sums_ref[rows, :] + added)
-
-    swap(3).wait()
-
     @pl.loop(0, 2)
     def _(turn):
-        half = (turn + y) % 2
-        rows = pl.ds(pl.multiple_of(half * 256, 256), 256)
-        done = sums_ref[rows, :] + add_part(3, half)
+        half = wrap(turn + y, 2)
+
+        @pl.loop(0, 4)
+        def _(part):
+            pl.when(turn == 0)(lambda: swap(part).wait())
+            added = add_part(part, half)
+            sums_ref[...] = jnp.where(part == 0, added, sums_ref[...] + added)
+
         for n in range(4):
-            rows32_ref[pl.ds(half * 1024 + n, 256, stride=4), :] = done[:, n * 128 : n * 128 + 128]
-
-        @pl.loop(0, 64)
+            rows32_ref[pl.ds(n, 256, stride=4), :] = sums_ref[:, n * 128 : n * 128 + 128]
+
+        @pl.loop(0, 16)
         def _(i):
-            to_x = 2 * half + (x + i) % 2
-            to_y = (y + i // 2 + i) % 4
-            to_z = (z + i // 8 + i) % 4
-            shard = (to_z * 4 + to_y) * 2 + (core + i // 32) % 2
-            owner = to_x * 32 + shard
-            part = rows32_ref[pl.ds(pl.multiple_of(owner * 16, 16), 16), :].astype(jnp.bfloat16)
-            parts_ref[owner] = part
-
-            @pl.when(owner != me)
-            def _():
-                copy_to(parts_ref.at[owner], recv_ref.at[mine], part_send, part_recv, (to_x, shard)).start()
+            for n in range(4):
+                to_x = 2 * half + wrap(x + n, 2)
+                to_y = wrap(y + i + 2 * (n // 2), 4)
+                to_z = wrap(z + i // 4 + i + n, 4)
+                shard = (to_z * 4 + to_y) * 2 + wrap(core + n // 2, 2)
+                owner = to_x * 32 + shard
+                at = pl.multiple_of((owner - 64 * half) * 16, 16)
+                parts_ref[owner] = rows32_ref[pl.ds(at, 16), :].astype(jnp.bfloat16)
+
+                @pl.when(owner != me)
+                def _():
+                    copy_to(parts_ref.at[owner], recv_ref.at[mine], part_send, part_recv, (to_x, shard)).start()
 
     recv_ref[mine] = parts_ref[me]
     copy_to(parts_ref.at[others], recv_ref.at[others], part_send, part_recv, somewhere).wait()
@@ -426,13 +431,12 @@
             pltpu.VMEM((QT, 256, 256), bf16),
             pltpu.VMEM((2, HALF, NT), bf16),
             pltpu.VMEM((QT, WIDE, 256), bf16),
-            pltpu.VMEM((2, WIDE, 128), f32),
-            pltpu.VMEM((2, WIDE, 128), f32),
+            pltpu.VMEM((QT, 2, WIDE, 128), f32),
             pltpu.VMEM((NB, 128), f32),
             pltpu.VMEM((QT, 40, 128), f32),
-            pltpu.VMEM((QT, 2, BLK, 128), f32),
-            pltpu.VMEM((QT, BLK, 128), f32),
-            pltpu.VMEM((5, BLK, 128), f32),
+            pltpu.VMEM((QT, 2, CHUNK, 128), f32),
+            pltpu.VMEM((QT, CHUNK, 128), f32),
+            pltpu.VMEM((5, CHUNK, 128), f32),
             pltpu.VMEM((3, QT, 128), f32),
             pltpu.VMEM((32 * BLK, 128), f32),
             pltpu.VMEM((NDEV, 32, 128), bf16),
@@ -441,7 +445,7 @@
             pltpu.VMEM((QT, NDEV, 256), bf16),
             pltpu.VMEM((2, PAIRS, NDEV), bf16),
             pltpu.VMEM((256, 1024), bf16),
-            pltpu.VMEM((PAIRS, NLAG), f32),
+            pltpu.VMEM((PAIRS // 2, NLAG), f32),
             pltpu.VMEM((NDEV, 16, 128), bf16),
             pltpu.VMEM((NDEV, 16, 128), bf16),
             pltpu.VMEM((QT, 256, NLAG), bf16),
@@ -464,7 +468,8 @@
 
 def body(samples, fan_taps, pair_blocks, pair_valid, coil_offsets):
     table = jnp.asarray(second_stage_table())
-    return correlate(pair_blocks.T, coil_offsets, pair_valid, samples.reshape(BLK, NT), fan_taps, table)
+    operands = (pair_blocks.T, coil_offsets, pair_valid, samples.reshape(BLK, NT), fan_taps, table)
+    return correlate(*(pltpu.with_memory_space_constraint(operand, pltpu.HBM) for operand in operands))
 
 
 def solution(mesh):

time: 71.1 us -> 60.4 us (0.85)
  local copies, waits for them, and re-layouts: 6.76 us -> 0.97 us
  Pallas kernels: 64 us -> 59.3 us
    unnamed x13 -> x1, local copies, waits for them, and re-layouts: 6.76 us -> 0.97 us
    pallas_call x1, Pallas kernels: 64 us -> 59.3 us  [correlate(): pl.pallas_call(kernel, out_shape=jax.ShapeDtypeStruct((4, BLK, NLAG), f32...]
where the time goes in v5:
time: 60.4 us; the launch traced here: 60.3 us
  Pallas kernels  59.3 us (98%)
  local copies, waits for them, and re-layouts  0.97 us (2%)
    pallas_call x1, Pallas kernels, correlate(): pl.pallas_call(kernel, out_shape=jax.ShapeDtypeStruct((4, BLK, NLAG), f32...  59.3 us

profile of v5, /device:TPU:1, one launch (start us, length us, event | category | flops | bytes accessed | tf_op | source)
XLA Modules:
  0.0 60.3 jit_solution(14843127384322185043)
XLA Ops:
  0.0 59.3 %correlate.1 = f32[4,128,512]{2,1,0:T(8,128)S(1)} custom-call(s32[2,512]{1,0:T(2,128)} %bitcast.3, s32[128]{0:T(128)} %offsets_hbm.1, s32[4]{0:T(128)} %valid_hbm.1, bf16[128,4096]{1,0:T(8,128)(2,1)} %bitcast.2, f32[33,2048]{1,0:T(8,128)} %fan_hbm.1, bf16[16,256,256]{2,1,0:T(8,128)(2,1)} %constant.2.clone.table_hbm), custom_call_target="tpu_custom_call" | custom-call | tf_op jit(solution)/shard_map/correlate/pallas_call | solution.py:420
  59.3 1.0 %copy.8 = f32[4,128,512]{2,1,0:T(8,128)} copy(f32[4,128,512]{2,1,0:T(8,128)S(1)} %correlate.1) | data formatting | bytes 2097152

commit v6 on v5

--- a/solution.py
+++ b/solution.py
@@ -87,7 +87,7 @@
     return lax.rem(value, size)
 
 
-def signal_some(barrier, i):
+def signal_some(barrier, i, guard=True):
     x, z, y, core = place()
     there = (x + i // 4) % 4
     row = (z + i % 4) % 4 * 8
@@ -98,7 +98,7 @@
             def signal():
                 pl.semaphore_signal(barrier, inc=1, device_id=(there, shard), device_id_type=MESH)
 
-            if dy == 0 and dc == 0:
+            if guard and dy == 0 and dc == 0:
                 pl.when(i > 0)(signal)
             else:
                 signal()
@@ -148,12 +148,13 @@
         lags_ref[q, 128 + half : 192 + half] = (-(sin_a * cos_b + cos_a * sin_b)).astype(jnp.bfloat16)
 
 
-def pick_rows(pairs_ref, pick_ref):
+def pick_rows(planes, pairs_ref, pick_ref):
     block = lax.broadcasted_iota(jnp.int32, (128, 128), 0)
     for side in range(2):
-        for at in range(0, PAIRS, 128):
-            chosen = block == pairs_ref[side : side + 1, at : at + 128]
-            pick_ref[side, at : at + 128, :] = jnp.where(chosen, 1.0, 0.0).T.astype(jnp.bfloat16)
+        for n, plane in enumerate(planes):
+            at = pl.ds(pl.multiple_of(plane * 128, 128), 128)
+            chosen = block == pairs_ref[side : side + 1, at]
+            pick_ref[side, n * 128 : n * 128 + 128, :] = jnp.where(chosen, 1.0, 0.0).T.astype(jnp.bfloat16)
 
 
 def bin_rows(offset, rows_ref):
@@ -181,7 +182,7 @@
 def kernel(
     pairs_hbm, offsets_hbm, valid_hbm, x_hbm, fan_hbm, table_hbm, out_ref,
     pairs_ref, offsets_ref, valid_ref, x_ref, fan_ref, table_ref,
-    halo_ref, y_ref, spec_ref, turned_ref, taps_ref, filt_ref, upto_ref, run_ref, rows_ref,
+    halo_ref, y_ref, y_halo_ref, spec_ref, turned_ref, taps_ref, filt_ref, upto_ref, run_ref, rows_ref,
     rows32_ref, white_ref, blocks_ref, own_ref, other_ref, pick_ref, cross_ref, sums_ref,
     parts_ref, recv_ref, lags_ref, coarse_ref, fine_ref,
     fetch_sem, halo_send, halo_recv, block_send, block_recv, swap_send, swap_recv, part_send, part_recv,
@@ -196,29 +197,31 @@
     fetches = [pltpu.make_async_copy(src, dst, fetch_sem.at[n]) for n, (src, dst) in enumerate(moves)]
     for fetch in fetches:
         fetch.start()
+
+    @pl.loop(0, 8)
+    def _(column):
+        signal_some(barrier, column)
+
     fetches[0].wait()
 
     @pl.loop(0, 8)
     def _(chunk):
-        signal_some(barrier, 2 * chunk)
-        signal_some(barrier, 2 * chunk + 1)
+        signal_some(barrier, chunk + 8, False)
         at = pl.ds(pl.multiple_of(chunk * 16, 16), 16)
-        to = pl.ds(pl.multiple_of(chunk * 16 + 16, 16), 16)
-        first_stage([x_ref[at, a * 128 : (a + 1) * 128].astype(jnp.float32) for a in range(32)], y_ref, to)
+        first_stage([x_ref[at, a * 128 : (a + 1) * 128].astype(jnp.float32) for a in range(32)], y_ref, at)
 
     for fetch in fetches[1:]:
         fetch.wait()
     sort_taps(fan_ref, turned_ref, taps_ref)
     bin_rows(offsets_ref[me], rows_ref)
 
-    def second_stage(rows):
-        @pl.loop(0, QT)
-        def _(q):
-            both = jnp.dot(y_ref[q, rows], table_ref[q], preferred_element_type=jnp.float32)
-            spec_ref[q, 0, rows] = both[:, :128]
-            spec_ref[q, 1, rows] = both[:, 128:]
-
-    second_stage(pl.ds(HALF, BLK))
+    @pl.loop(0, QT // 4)
+    def _(group):
+        for n in range(4):
+            q = group * 4 + n
+            both = jnp.dot(y_ref[q], table_ref[q], preferred_element_type=jnp.float32)
+            spec_ref[q, 0, HALF : HALF + BLK] = both[:, :128]
+            spec_ref[q, 1, HALF : HALF + BLK] = both[:, 128:]
 
     pl.semaphore_wait(barrier, NDEV - 1)
     after, before = wrap(me + 1, NDEV), wrap(me + NDEV - 1, NDEV)
@@ -240,15 +243,21 @@
         @pl.loop(0, 2)
         def _(side):
             edge = jnp.where(side == 0, me > 0, me < NDEV - 1).astype(jnp.float32)
-            to = pl.ds(pl.multiple_of(side * (BLK + HALF), 16), 16)
+            to = pl.ds(pl.multiple_of(side * HALF, HALF), HALF)
             first_stage(
                 [halo_ref[side, :, a * 128 : (a + 1) * 128].astype(jnp.float32) * edge for a in range(32)],
-                y_ref,
+                y_halo_ref,
                 to,
             )
 
-        second_stage(pl.ds(0, HALF))
-        second_stage(pl.ds(BLK + HALF, HALF))
+        @pl.loop(0, QT // 4)
+        def _(group):
+            for n in range(4):
+                q = group * 4 + n
+                both = jnp.dot(y_halo_ref[q], table_ref[q], preferred_element_type=jnp.float32)
+                for r in range(2):
+                    spec_ref[q, r, 0:HALF] = both[:HALF, r * 128 : r * 128 + 128]
+                    spec_ref[q, r, HALF + BLK : WIDE] = both[HALF:, r * 128 : r * 128 + 128]
 
     lanes = lax.broadcasted_iota(jnp.int32, (CHUNK, 128), 1)
     low = lanes < 64
@@ -257,6 +266,9 @@
     mine = channel_of(x, z, y, core)
     somewhere = (x, lax.axis_index("shard") + 1 - 2 * core)
     others = pl.ds(0, NDEV - 1)
+    xs = [wrap(x + 4 + sign * n, 4) for n in range(4)]
+    zs = [wrap(z + 4 + sign * n, 4) for n in range(4)]
+    ys = [wrap(y // 2 + n, 2) for n in range(2)]
 
     @pl.loop(0, 4)
     def _(turn):
@@ -312,29 +324,23 @@
             rows32_ref[pl.ds(16 + q, CHUNK, stride=32), :] = (im * cos - re * sin) * scale
 
         to_core, parity = chunk // 2, wrap(chunk, 2)
-
-        @pl.loop(0, 8)
-        def _(i):
-            to_y2 = wrap(y // 2 + i // 4, 2)
-            for dx in range(4):
-                to_x = wrap(x + 4 + sign * dx, 4)
-                to_z = wrap(z + 4 + sign * wrap(i + dx, 4), 4)
-                to_y = 2 * to_y2 + wrap(parity + to_x + to_z, 2)
-                shard = (to_z * 4 + to_y) * 2 + to_core
-                channel = channel_of(to_x, to_z, to_y, to_core)
-                at = pl.multiple_of((channel - first) * 32, 32)
-                white_ref[channel] = rows32_ref[pl.ds(at, 32), :].astype(jnp.bfloat16)
-
-                @pl.when(channel != mine)
-                def _():
-                    copy_to(
-                        white_ref.at[channel], blocks_ref.at[me], block_send, block_recv, (to_x, shard)
-                    ).start()
+        for n in range(32):
+            to_x, to_z, to_y2 = xs[n % 4], zs[(n // 4 + n) % 4], ys[n // 16]
+            shard = to_z * 8 + to_y2 * 4 + 2 * wrap(parity + to_x + to_z, 2) + to_core
+            row = to_x * 8 + to_z * 2 + to_y2
+            white_ref[first + row] = rows32_ref[pl.ds(pl.multiple_of(row * 32, 32), 32), :].astype(jnp.bfloat16)
+            push = copy_to(
+                white_ref.at[first + row], blocks_ref.at[me], block_send, block_recv, (to_x, shard)
+            ).start
+            if n == 0:
+                pl.when(first + row != mine)(push)
+            else:
+                push()
 
     blocks_ref[me] = white_ref[mine]
 
     lag_tables(coarse_ref, fine_ref)
-    pick_rows(pairs_ref, pick_ref)
+    pick_rows(xs, pairs_ref, pick_ref)
 
     @pl.loop(0, QT)
     def _(q):
@@ -374,33 +380,34 @@
 
     @pl.loop(0, 2)
     def _(turn):
-        half = wrap(turn + y, 2)
-
         @pl.loop(0, 4)
         def _(part):
             pl.when(turn == 0)(lambda: swap(part).wait())
-            added = add_part(part, half)
+            added = add_part(part, turn)
             sums_ref[...] = jnp.where(part == 0, added, sums_ref[...] + added)
 
         for n in range(4):
             rows32_ref[pl.ds(n, 256, stride=4), :] = sums_ref[:, n * 128 : n * 128 + 128]
 
-        @pl.loop(0, 16)
+        planes = [wrap(x + 4 + sign * (2 * turn + n), 4) for n in range(2)]
+
+        @pl.loop(0, 4)
         def _(i):
-            for n in range(4):
-                to_x = 2 * half + wrap(x + n, 2)
-                to_y = wrap(y + i + 2 * (n // 2), 4)
-                to_z = wrap(z + i // 4 + i + n, 4)
-                shard = (to_z * 4 + to_y) * 2 + wrap(core + n // 2, 2)
-                owner = to_x * 32 + shard
-                at = pl.multiple_of((owner - 64 * half) * 16, 16)
-                parts_ref[owner] = rows32_ref[pl.ds(at, 16), :].astype(jnp.bfloat16)
-
-                @pl.when(owner != me)
-                def _():
-                    copy_to(parts_ref.at[owner], recv_ref.at[mine], part_send, part_recv, (to_x, shard)).start()
-
-    recv_ref[mine] = parts_ref[me]
+            for n in range(16):
+                to_core = core if n < 8 else 1 - core
+                shard = zs[n // 2 % 4] * 8 + wrap(y + i + n, 4) * 2 + to_core
+                row = n % 2 * 32 + shard
+                slot = turn * 64 + row
+                parts_ref[slot] = rows32_ref[pl.ds(pl.multiple_of(row * 16, 16), 16), :].astype(jnp.bfloat16)
+                push = copy_to(
+                    parts_ref.at[slot], recv_ref.at[mine], part_send, part_recv, (planes[n % 2], shard)
+                ).start
+                if n == 0:
+                    pl.when(turn + i > 0)(push)
+                else:
+                    push()
+
+    recv_ref[mine] = parts_ref[lax.axis_index("shard")]
     copy_to(parts_ref.at[others], recv_ref.at[others], part_send, part_recv, somewhere).wait()
 
     @pl.loop(0, NDEV // 16)
@@ -430,7 +437,8 @@
             pltpu.VMEM((TAPS, NB), f32),
             pltpu.VMEM((QT, 256, 256), bf16),
             pltpu.VMEM((2, HALF, NT), bf16),
-            pltpu.VMEM((QT, WIDE, 256), bf16),
+            pltpu.VMEM((QT, BLK, 256), bf16),
+            pltpu.VMEM((QT, 2 * HALF, 256), bf16),
             pltpu.VMEM((QT, 2, WIDE, 128), f32),
             pltpu.VMEM((NB, 128), f32),
             pltpu.VMEM((QT, 40, 128), f32),

time: 60.4 us -> 50.8 us (0.84)
  Pallas kernels: 59.3 us -> 49.7 us
    pallas_call x1, Pallas kernels: 59.3 us -> 49.7 us  [correlate(): pl.pallas_call(kernel, out_shape=jax.ShapeDtypeStruct((4, BLK, NLAG), f32...]
where the time goes in v6:
time: 50.8 us; the launch traced here: 50.7 us
  Pallas kernels  49.7 us (98%)
  local copies, waits for them, and re-layouts  0.97 us (2%)
    pallas_call x1, Pallas kernels, correlate(): pl.pallas_call(kernel, out_shape=jax.ShapeDtypeStruct((4, BLK, NLAG), f32...  49.7 us

profile of v6, /device:TPU:1, one launch (start us, length us, event | category | flops | bytes accessed | tf_op | source)
XLA Modules:
  0.0 50.7 jit_solution(6274616687804723425)
XLA Ops:
  0.0 49.7 %correlate.1 = f32[4,128,512]{2,1,0:T(8,128)S(1)} custom-call(s32[2,512]{1,0:T(2,128)} %bitcast.3, s32[128]{0:T(128)} %offsets_hbm.1, s32[4]{0:T(128)} %valid_hbm.1, bf16[128,4096]{1,0:T(8,128)(2,1)} %bitcast.2, f32[33,2048]{1,0:T(8,128)} %fan_hbm.1, bf16[16,256,256]{2,1,0:T(8,128)(2,1)} %constant.2.clone.table_hbm), custom_call_target="tpu_custom_call" | custom-call | tf_op jit(solution)/shard_map/correlate/pallas_call | solution.py:427
  49.7 1.0 %copy.8 = f32[4,128,512]{2,1,0:T(8,128)} copy(f32[4,128,512]{2,1,0:T(8,128)S(1)} %correlate.1) | data formatting | bytes 2097152

commit v7 on v6

--- a/solution.py
+++ b/solution.py
@@ -320,15 +320,15 @@
             scale = lax.rsqrt(window * rows_ref[2, pl.ds(q, 1), :] + EPSILON)
             cos = rows_ref[0, pl.ds(q, 1), :]
             sin = rows_ref[1, pl.ds(q, 1), :]
-            rows32_ref[pl.ds(q, CHUNK, stride=32), :] = (re * cos + im * sin) * scale
-            rows32_ref[pl.ds(16 + q, CHUNK, stride=32), :] = (im * cos - re * sin) * scale
+            rows32_ref[pl.ds(q, CHUNK, stride=33), :] = (re * cos + im * sin) * scale
+            rows32_ref[pl.ds(16 + q, CHUNK, stride=33), :] = (im * cos - re * sin) * scale
 
         to_core, parity = chunk // 2, wrap(chunk, 2)
         for n in range(32):
             to_x, to_z, to_y2 = xs[n % 4], zs[(n // 4 + n) % 4], ys[n // 16]
             shard = to_z * 8 + to_y2 * 4 + 2 * wrap(parity + to_x + to_z, 2) + to_core
             row = to_x * 8 + to_z * 2 + to_y2
-            white_ref[first + row] = rows32_ref[pl.ds(pl.multiple_of(row * 32, 32), 32), :].astype(jnp.bfloat16)
+            white_ref[first + row] = rows32_ref[pl.ds(row * 33, 32), :].astype(jnp.bfloat16)
             push = copy_to(
                 white_ref.at[first + row], blocks_ref.at[me], block_send, block_recv, (to_x, shard)
             ).start
@@ -350,9 +350,8 @@
 
     @pl.loop(0, NDEV // 8)
     def _(d):
-        eight = pl.ds(pl.multiple_of(d * 8, 8), 8)
-        to = pl.ds(pl.multiple_of(d * 256, 256), 256)
-        rows32_ref[to, :] = blocks_ref[eight].reshape(256, 128).astype(jnp.float32)
+        for n in range(8):
+            rows32_ref[pl.ds((d * 8 + n) * 33, 32), :] = blocks_ref[d * 8 + n].astype(jnp.float32)
 
     def swap(part):
         some = pl.ds(part * 4, 4)
@@ -362,8 +361,8 @@
     def _(part):
         for n in range(4):
             q = part * 4 + n
-            own_ref[q, :, 0:128] = rows32_ref[pl.ds(q, BLK, stride=32), :].astype(jnp.bfloat16)
-            own_ref[q, :, 128:256] = rows32_ref[pl.ds(16 + q, BLK, stride=32), :].astype(jnp.bfloat16)
+            own_ref[q, :, 0:128] = rows32_ref[pl.ds(q, BLK, stride=33), :].astype(jnp.bfloat16)
+            own_ref[q, :, 128:256] = rows32_ref[pl.ds(16 + q, BLK, stride=33), :].astype(jnp.bfloat16)
         swap(part).start()
 
     def add_part(part, half):
@@ -412,14 +411,13 @@
 
     @pl.loop(0, NDEV // 16)
     def _(d):
-        some = pl.ds(pl.multiple_of(d * 16, 16), 16)
-        to = pl.ds(pl.multiple_of(d * 256, 256), 256)
-        rows32_ref[to, :] = recv_ref[some].reshape(256, 128).astype(jnp.float32)
+        for n in range(16):
+            rows32_ref[pl.ds((d * 16 + n) * 17, 16), :] = recv_ref[d * 16 + n].astype(jnp.float32)
 
     for p in range(4):
         weight = valid_ref[p].astype(jnp.float32) * (1.0 / math.sqrt(NB))
         for n in range(4):
-            out_ref[p, :, n * 128 : n * 128 + 128] = rows32_ref[pl.ds(p * 4 + n, BLK, stride=16), :] * weight
+            out_ref[p, :, n * 128 : n * 128 + 128] = rows32_ref[pl.ds(p * 4 + n, BLK, stride=17), :] * weight
 
 
 def correlate(*operands):
@@ -446,7 +444,7 @@
             pltpu.VMEM((QT, CHUNK, 128), f32),
             pltpu.VMEM((5, CHUNK, 128), f32),
             pltpu.VMEM((3, QT, 128), f32),
-            pltpu.VMEM((32 * BLK, 128), f32),
+            pltpu.VMEM((33 * BLK, 128), f32),
             pltpu.VMEM((NDEV, 32, 128), bf16),
             pltpu.VMEM((NDEV, 32, 128), bf16),
             pltpu.VMEM((QT, NDEV, 256), bf16),

time: 50.8 us -> 49.3 us (0.970)
  Pallas kernels: 49.7 us -> 48.2 us
    pallas_call x1, Pallas kernels: 49.7 us -> 48.2 us  [correlate(): pl.pallas_call(kernel, out_shape=jax.ShapeDtypeStruct((4, BLK, NLAG), f32...]
where the time goes in v7:
time: 49.3 us; the launch traced here: 49.2 us
  Pallas kernels  48.2 us (98%)
  local copies, waits for them, and re-layouts  0.97 us (2%)
    pallas_call x1, Pallas kernels, correlate(): pl.pallas_call(kernel, out_shape=jax.ShapeDtypeStruct((4, BLK, NLAG), f32...  48.2 us

profile of v7, /device:TPU:1, one launch (start us, length us, event | category | flops | bytes accessed | tf_op | source)
XLA Modules:
  0.0 49.2 jit_solution(11875095843377246294)
XLA Ops:
  0.0 48.2 %correlate.1 = f32[4,128,512]{2,1,0:T(8,128)S(1)} custom-call(s32[2,512]{1,0:T(2,128)} %bitcast.3, s32[128]{0:T(128)} %offsets_hbm.1, s32[4]{0:T(128)} %valid_hbm.1, bf16[128,4096]{1,0:T(8,128)(2,1)} %bitcast.2, f32[33,2048]{1,0:T(8,128)} %fan_hbm.1, bf16[16,256,256]{2,1,0:T(8,128)(2,1)} %constant.2.clone.table_hbm), custom_call_target="tpu_custom_call" | custom-call | tf_op jit(solution)/shard_map/correlate/pallas_call | solution.py:425
  48.2 1.0 %copy.8 = f32[4,128,512]{2,1,0:T(8,128)} copy(f32[4,128,512]{2,1,0:T(8,128)S(1)} %correlate.1) | data formatting | bytes 2097152

commit v8 on v7

--- a/solution.py
+++ b/solution.py
@@ -290,7 +290,7 @@
             upto_ref[q] = run
             return run
 
-        run = lax.fori_loop(0, QT, fan, jnp.zeros((CHUNK, 128), jnp.float32))
+        run = lax.fori_loop(0, QT, fan, jnp.zeros((CHUNK, 128), jnp.float32), unroll=2)
 
         power = filt_ref[0, 0] * filt_ref[0, 0] + filt_ref[0, 1] * filt_ref[0, 1]
         sums = run + jnp.where(low, 0.0, power)
@@ -305,7 +305,7 @@
         run_ref[3] = jnp.where(low, power, sums)
         run_ref[4] = jnp.where(low, total, swapped + power)
 
-        @pl.loop(0, QT, unroll=2)
+        @pl.loop(0, QT, unroll=8)
         def _(q):
             re, im = filt_ref[q, 0], filt_ref[q, 1]
             upto = jnp.where(q == 0, run_ref[3], upto_ref[q])

time: 49.3 us -> 47.3 us (0.959)
  Pallas kernels: 48.2 us -> 46.3 us
    pallas_call x1, Pallas kernels: 48.2 us -> 46.3 us  [correlate(): pl.pallas_call(kernel, out_shape=jax.ShapeDtypeStruct((4, BLK, NLAG), f32...]
where the time goes in v8:
time: 47.3 us; the launch traced here: 47.2 us
  Pallas kernels  46.3 us (98%)
  local copies, waits for them, and re-layouts  0.97 us (2%)
    pallas_call x1, Pallas kernels, correlate(): pl.pallas_call(kernel, out_shape=jax.ShapeDtypeStruct((4, BLK, NLAG), f32...  46.3 us
    unnamed x1, local copies, waits for them, and re-layouts  0.97 us

profile of v8, /device:TPU:1, one launch (start us, length us, event | category | flops | bytes accessed | tf_op | source)
XLA Modules:
  0.0 47.2 jit_solution(16740014425908083814)
XLA Ops:
  0.0 46.3 %correlate.1 = f32[4,128,512]{2,1,0:T(8,128)S(1)} custom-call(s32[2,512]{1,0:T(2,128)} %bitcast.3, s32[128]{0:T(128)} %offsets_hbm.1, s32[4]{0:T(128)} %valid_hbm.1, bf16[128,4096]{1,0:T(8,128)(2,1)} %bitcast.2, f32[33,2048]{1,0:T(8,128)} %fan_hbm.1, bf16[16,256,256]{2,1,0:T(8,128)(2,1)} %constant.2.clone.table_hbm), custom_call_target="tpu_custom_call" | custom-call | tf_op jit(solution)/shard_map/correlate/pallas_call | solution.py:425
  46.3 1.0 %copy.8 = f32[4,128,512]{2,1,0:T(8,128)} copy(f32[4,128,512]{2,1,0:T(8,128)S(1)} %correlate.1) | data formatting | bytes 2097152

commit v9 on v8

--- a/solution.py
+++ b/solution.py
@@ -348,7 +348,7 @@
 
     copy_to(white_ref.at[others], blocks_ref.at[others], block_send, block_recv, somewhere).wait()
 
-    @pl.loop(0, NDEV // 8)
+    @pl.loop(0, NDEV // 8, unroll=2)
     def _(d):
         for n in range(8):
             rows32_ref[pl.ds((d * 8 + n) * 33, 32), :] = blocks_ref[d * 8 + n].astype(jnp.float32)
@@ -390,7 +390,7 @@
 
         planes = [wrap(x + 4 + sign * (2 * turn + n), 4) for n in range(2)]
 
-        @pl.loop(0, 4)
+        @pl.loop(0, 4, unroll=2)
         def _(i):
             for n in range(16):
                 to_core = core if n < 8 else 1 - core
@@ -438,13 +438,13 @@
             pltpu.VMEM((QT, BLK, 256), bf16),
             pltpu.VMEM((QT, 2 * HALF, 256), bf16),
             pltpu.VMEM((QT, 2, WIDE, 128), f32),
-            pltpu.VMEM((NB, 128), f32),
+            pltpu.VMEM((NB + 64, 128), f32),
             pltpu.VMEM((QT, 40, 128), f32),
             pltpu.VMEM((QT, 2, CHUNK, 128), f32),
             pltpu.VMEM((QT, CHUNK, 128), f32),
             pltpu.VMEM((5, CHUNK, 128), f32),
             pltpu.VMEM((3, QT, 128), f32),
-            pltpu.VMEM((33 * BLK, 128), f32),
+            pltpu.VMEM((33 * BLK + 64, 128), f32),
             pltpu.VMEM((NDEV, 32, 128), bf16),
             pltpu.VMEM((NDEV, 32, 128), bf16),
             pltpu.VMEM((QT, NDEV, 256), bf16),

time: 47.3 us -> 47.3 us (level)
  no operation moved by 1% of the time
where the time goes in v9:
time: 47.3 us; the launch traced here: 47.2 us
  Pallas kernels  46.2 us (98%)
  local copies, waits for them, and re-layouts  0.97 us (2%)
    pallas_call x1, Pallas kernels, correlate(): pl.pallas_call(kernel, out_shape=jax.ShapeDtypeStruct((4, BLK, NLAG), f32...  46.2 us
    unnamed x1, local copies, waits for them, and re-layouts  0.97 us

profile of v9, /device:TPU:1, one launch (start us, length us, event | category | flops | bytes accessed | tf_op | source)
XLA Modules:
  0.0 47.2 jit_solution(3557215833395758197)
XLA Ops:
  0.0 46.2 %correlate.1 = f32[4,128,512]{2,1,0:T(8,128)S(1)} custom-call(s32[2,512]{1,0:T(2,128)} %bitcast.3, s32[128]{0:T(128)} %offsets_hbm.1, s32[4]{0:T(128)} %valid_hbm.1, bf16[128,4096]{1,0:T(8,128)(2,1)} %bitcast.2, f32[33,2048]{1,0:T(8,128)} %fan_hbm.1, bf16[16,256,256]{2,1,0:T(8,128)(2,1)} %constant.2.clone.table_hbm), custom_call_target="tpu_custom_call" | custom-call | tf_op jit(solution)/shard_map/correlate/pallas_call | solution.py:425
  46.2 1.0 %copy.8 = f32[4,128,512]{2,1,0:T(8,128)} copy(f32[4,128,512]{2,1,0:T(8,128)S(1)} %correlate.1) | data formatting | bytes 2097152

commit v10 on v9

--- a/solution.py
+++ b/solution.py
@@ -240,7 +240,7 @@
         to_after.wait()
         to_before.wait()
 
-        @pl.loop(0, 2)
+        @pl.loop(0, 2, unroll=2)
         def _(side):
             edge = jnp.where(side == 0, me > 0, me < NDEV - 1).astype(jnp.float32)
             to = pl.ds(pl.multiple_of(side * HALF, HALF), HALF)
@@ -250,7 +250,7 @@
                 to,
             )
 
-        @pl.loop(0, QT // 4)
+        @pl.loop(0, QT // 4, unroll=2)
         def _(group):
             for n in range(4):
                 q = group * 4 + n

time: 47.3 us -> 47.2 us (level)
  no operation moved by 1% of the time
where the time goes in v10:
time: 47.2 us; the launch traced here: 47.1 us
  Pallas kernels  46.2 us (98%)
  local copies, waits for them, and re-layouts  0.97 us (2%)
    pallas_call x1, Pallas kernels, correlate(): pl.pallas_call(kernel, out_shape=jax.ShapeDtypeStruct((4, BLK, NLAG), f32...  46.2 us
    unnamed x1, local copies, waits for them, and re-layouts  0.97 us

profile of v10, /device:TPU:1, one launch (start us, length us, event | category | flops | bytes accessed | tf_op | source)
XLA Modules:
  0.0 47.1 jit_solution(6547889264482102306)
XLA Ops:
  0.0 46.2 %correlate.1 = f32[4,128,512]{2,1,0:T(8,128)S(1)} custom-call(s32[2,512]{1,0:T(2,128)} %bitcast.3, s32[128]{0:T(128)} %offsets_hbm.1, s32[4]{0:T(128)} %valid_hbm.1, bf16[128,4096]{1,0:T(8,128)(2,1)} %bitcast.2, f32[33,2048]{1,0:T(8,128)} %fan_hbm.1, bf16[16,256,256]{2,1,0:T(8,128)(2,1)} %constant.2.clone.table_hbm), custom_call_target="tpu_custom_call" | custom-call | tf_op jit(solution)/shard_map/correlate/pallas_call | solution.py:425
  46.2 1.0 %copy.8 = f32[4,128,512]{2,1,0:T(8,128)} copy(f32[4,128,512]{2,1,0:T(8,128)S(1)} %correlate.1) | data formatting | bytes 2097152

commit v11 on v9

--- a/solution.py
+++ b/solution.py
@@ -357,7 +357,7 @@
         some = pl.ds(part * 4, 4)
         return copy_to(own_ref.at[some], other_ref.at[some], swap_send.at[part], swap_recv.at[part], somewhere)
 
-    @pl.loop(0, 4)
+    @pl.loop(0, 4, unroll=2)
     def _(part):
         for n in range(4):
             q = part * 4 + n

time: 47.3 us -> 47.3 us (level)
  no operation moved by 1% of the time
where the time goes in v11:
time: 47.3 us; the launch traced here: 47.2 us
  Pallas kernels  46.2 us (98%)
  local copies, waits for them, and re-layouts  0.97 us (2%)
    pallas_call x1, Pallas kernels, correlate(): pl.pallas_call(kernel, out_shape=jax.ShapeDtypeStruct((4, BLK, NLAG), f32...  46.2 us
    unnamed x1, local copies, waits for them, and re-layouts  0.97 us

profile of v11, /device:TPU:1, one launch (start us, length us, event | category | flops | bytes accessed | tf_op | source)
XLA Modules:
  0.0 47.2 jit_solution(3305658339427205469)
XLA Ops:
  0.0 46.2 %correlate.1 = f32[4,128,512]{2,1,0:T(8,128)S(1)} custom-call(s32[2,512]{1,0:T(2,128)} %bitcast.3, s32[128]{0:T(128)} %offsets_hbm.1, s32[4]{0:T(128)} %valid_hbm.1, bf16[128,4096]{1,0:T(8,128)(2,1)} %bitcast.2, f32[33,2048]{1,0:T(8,128)} %fan_hbm.1, bf16[16,256,256]{2,1,0:T(8,128)(2,1)} %constant.2.clone.table_hbm), custom_call_target="tpu_custom_call" | custom-call | tf_op jit(solution)/shard_map/correlate/pallas_call | solution.py:425
  46.2 1.0 %copy.8 = f32[4,128,512]{2,1,0:T(8,128)} copy(f32[4,128,512]{2,1,0:T(8,128)S(1)} %correlate.1) | data formatting | bytes 2097152
